TPU v7x, 512 devices: a whole 4x4x16 slice. The times are simulated.
512 devices in a mesh: rep: 4 (over y), shard: 32 (over z, core), tp: 4 (over x).
Axes of the slice: x: 4, y: 4, z: 16, core: 2. Of those that a mesh axis runs over, the one named last changes fastest.
Arguments:
- qkv_grad: bfloat16 [4, 1024, 3072], P('rep', 'shard', 'tp'), may hold values from -100 to 100
- qkv_error: float32 [4, 1024, 3072], P('rep', 'shard', 'tp'), may hold values from -4 to 4
- qkv_basis: float32 [3072, 32], P('tp'), may hold values from -6 to 6
- qkv_weight: float32 [32, 4, 8, 3072], P('shard', 'rep', None, 'tp'), may hold values from -0.75 to 0.75
- qkv_moment: float32 [32, 4, 8, 3072], P('shard', 'rep', None, 'tp'), may hold values from -0.75 to 0.75
- gu_grad: bfloat16 [4, 1024, 8192], P('rep', 'shard', 'tp'), may hold values from -100 to 100
- gu_error: float32 [4, 1024, 8192], P('rep', 'shard', 'tp'), may hold values from -4 to 4
- gu_basis: float32 [8192, 32], P('tp'), may hold values from -6 to 6
- gu_weight: float32 [32, 4, 8, 8192], P('shard', 'rep', None, 'tp'), may hold values from -0.75 to 0.75
- gu_moment: float32 [32, 4, 8, 8192], P('shard', 'rep', None, 'tp'), may hold values from -0.75 to 0.75
- down_grad: bfloat16 [4, 4096, 1024], P('rep', 'shard', 'tp'), may hold values from -100 to 100
- down_error: float32 [4, 4096, 1024], P('rep', 'shard', 'tp'), may hold values from -4 to 4
- down_basis: float32 [1024, 32], P('tp'), may hold values from -6 to 6
- down_weight: float32 [32, 4, 32, 1024], P('shard', 'rep', None, 'tp'), may hold values from -0.75 to 0.75
- down_moment: float32 [32, 4, 32, 1024], P('shard', 'rep', None, 'tp'), may hold values from -0.75 to 0.75
- vec_grad: bfloat16 [4, 11264], P('rep', ('shard', 'tp')), may hold values from -6 to 6
- vec_weight: float32 [11264], P(('shard', 'tp')), may hold values from 0.5 to 1.5
- vec_moment: float32 [11264], P(('shard', 'tp')), may hold values from -6 to 6
- emb_ids: int32 [4, 4096], P('rep', 'shard'), may hold values from 0 to 31999
- emb_grad: bfloat16 [4, 4096, 1024], P('rep', 'shard', 'tp'), may hold values from -6 to 6
- emb_weight: float32 [32, 4, 250, 1024], P('shard', 'rep', None, 'tp'), may hold values from -0.75 to 0.75
- emb_moment: float32 [32, 4, 250, 1024], P('shard', 'rep', None, 'tp'), may hold values from -6 to 6
Outputs:
- qkv_new: float32 [1024, 3072], P('shard', 'tp')
- qkv_error_new: float32 [4, 1024, 3072], P('rep', 'shard', 'tp')
- qkv_moment_new: float32 [32, 4, 8, 3072], P('shard', 'rep', None, 'tp')
- gu_new: float32 [1024, 8192], P('shard', 'tp')
- gu_error_new: float32 [4, 1024, 8192], P('rep', 'shard', 'tp')
- gu_moment_new: float32 [32, 4, 8, 8192], P('shard', 'rep', None, 'tp')
- down_new: float32 [4096, 1024], P('shard', 'tp')
- down_error_new: float32 [4, 4096, 1024], P('rep', 'shard', 'tp')
- down_moment_new: float32 [32, 4, 32, 1024], P('shard', 'rep', None, 'tp')
- vec_new: float32 [11264], P(('shard', 'tp'))
- vec_moment_new: float32 [11264], P(('shard', 'tp'))
- emb_new: float32 [32000, 1024], P('shard', 'tp')
- emb_moment_new: float32 [32, 4, 250, 1024], P('shard', 'rep', None, 'tp')
All inputs are finite; a program needn't handle non-finite values.
Results may differ from a plain program's by a relative error of at most 0.0004.
Values may be sent and summed in bfloat16 or wider, within the bound.
A program may use at most 64 MiB of HBM per device.

v0:
```python
import jax
import jax.numpy as jnp
from jax import lax
from jax.sharding import PartitionSpec as P

ROUNDS = 2


momentum_decay = 0.9
step_size = 0.05


def solve_right(lower_factor, values):
    return jax.scipy.linalg.solve_triangular(lower_factor, values.T, lower=True).T


def dot_high(left_side, right_side):
    return jnp.dot(left_side, right_side, precision=lax.Precision.HIGHEST)


def add_rows(running, row_ids, row_values, row_start, block_rows):

    def one_block(partial_sum, block_ids, block_values):
        local_ids = block_ids - row_start
        one_hot = (
            local_ids[None, :]
            == lax.broadcasted_iota(jnp.int32, (block_rows, block_ids.shape[0]), 0)
        ).astype(jnp.bfloat16)
        return partial_sum + jnp.dot(one_hot, block_values, preferred_element_type=jnp.float32)

    count = row_ids.shape[0]
    width = 512
    split_ids = row_ids.reshape(count // width, width)
    split_values = row_values.reshape(count // width, width, row_values.shape[-1])

    def scan_step(partial_sum, inputs):
        return (one_block(partial_sum, inputs[0], inputs[1]), None)

    return lax.scan(scan_step, running, (split_ids, split_values))[0]


def on_device(
    qkv_grad,
    qkv_error,
    qkv_basis,
    qkv_weight,
    qkv_moment,
    gu_grad,
    gu_error,
    gu_basis,
    gu_weight,
    gu_moment,
    down_grad,
    down_error,
    down_basis,
    down_weight,
    down_moment,
    vec_grad,
    vec_weight,
    vec_moment,
    emb_ids,
    emb_grad,
    emb_weight,
    emb_moment,
):
    rep_count = lax.axis_size("rep")
    rep_index = lax.axis_index("rep")
    shard_index = lax.axis_index("shard")
    fulls = [
        qkv_grad[0].astype(jnp.float32) + qkv_error[0],
        gu_grad[0].astype(jnp.float32) + gu_error[0],
        down_grad[0].astype(jnp.float32) + down_error[0],
    ]
    rights = [qkv_basis, gu_basis, down_basis]
    lefts = rights
    for round_index in range(ROUNDS):
        parts = [
            dot_high(full_grad, right_factor) for full_grad, right_factor in zip(fulls, rights)
        ]
        lefts = [lax.psum(left_part, ("rep", "tp")) for left_part in parts]
        grams = [dot_high(left_factor.T, left_factor) for left_factor in lefts]
        summed = lax.psum((grams[0], grams[1], grams[2]), "shard")
        lowers = [jnp.linalg.cholesky(summed[index]) for index in range(3)]
        lefts = [solve_right(lowers[index], lefts[index]) for index in range(3)]
        raw_rights = [
            dot_high(full_grad.T, left_factor) for full_grad, left_factor in zip(fulls, lefts)
        ]
        rights = list(lax.psum((raw_rights[0], raw_rights[1], raw_rights[2]), ("rep", "shard")))
    errors_new = []
    moments_new = []
    flats_new = []
    for index, (weight, moment) in enumerate(
        ((qkv_weight, qkv_moment), (gu_weight, gu_moment), (down_weight, down_moment))
    ):
        approx = dot_high(lefts[index], rights[index].T) / rep_count
        errors_new.append((fulls[index] - approx)[None])
        local_rows = weight.shape[2]
        own_rows = lax.dynamic_slice_in_dim(approx, rep_index * local_rows, local_rows, 0)
        moment_new = momentum_decay * moment[0, 0] + own_rows
        moments_new.append(moment_new[None, None])
        flats_new.append((weight[0, 0] - step_size * moment_new)[None, None])
    vec_mean = lax.psum(vec_grad[0].astype(jnp.float32), "rep") / rep_count
    vec_moment_new = momentum_decay * vec_moment + vec_mean
    vec_new = vec_weight - step_size * vec_moment_new
    block_rows = emb_weight.shape[2]
    row_width = emb_grad.shape[2]
    row_start = (shard_index * rep_count + rep_index) * block_rows
    initial = jnp.zeros((block_rows, row_width), jnp.float32)
    pieces = (
        lax.all_gather(emb_ids, ("rep", "shard"), axis=1, tiled=True),
        lax.all_gather(emb_grad, ("rep", "shard"), axis=1, tiled=True),
    )
    row_ids = pieces[0].reshape(-1)
    row_values = pieces[1].reshape(-1, pieces[1].shape[-1])
    emb_sum = add_rows(initial, row_ids, row_values, row_start, block_rows) / rep_count
    emb_moment_new = momentum_decay * emb_moment[0, 0] + emb_sum
    emb_flat_new = (emb_weight[0, 0] - step_size * emb_moment_new)[None, None]
    gathered = (
        lax.all_gather(flats_new[0], "rep", axis=1, tiled=True),
        lax.all_gather(flats_new[1], "rep", axis=1, tiled=True),
        lax.all_gather(flats_new[2], "rep", axis=1, tiled=True),
        lax.all_gather(emb_flat_new, "rep", axis=1, tiled=True),
    )
    plains = [whole.reshape(whole.shape[1] * whole.shape[2], whole.shape[3]) for whole in gathered]
    return (
        plains[0],
        errors_new[0],
        moments_new[0],
        plains[1],
        errors_new[1],
        moments_new[1],
        plains[2],
        errors_new[2],
        moments_new[2],
        vec_new,
        vec_moment_new,
        plains[3],
        emb_moment_new[None, None],
    )


def solution(mesh):
    return jax.shard_map(
        on_device,
        mesh=mesh,
        in_specs=(
            P("rep", "shard", "tp"),
            P("rep", "shard", "tp"),
            P("tp", None),
            P("shard", "rep", None, "tp"),
            P("shard", "rep", None, "tp"),
            P("rep", "shard", "tp"),
            P("rep", "shard", "tp"),
            P("tp", None),
            P("shard", "rep", None, "tp"),
            P("shard", "rep", None, "tp"),
            P("rep", "shard", "tp"),
            P("rep", "shard", "tp"),
            P("tp", None),
            P("shard", "rep", None, "tp"),
            P("shard", "rep", None, "tp"),
            P("rep", ("shard", "tp")),
            P(("shard", "tp")),
            P(("shard", "tp")),
            P("rep", "shard"),
            P("rep", "shard", "tp"),
            P("shard", "rep", None, "tp"),
            P("shard", "rep", None, "tp"),
        ),
        out_specs=(
            P("shard", "tp"),
            P("rep", "shard", "tp"),
            P("shard", "rep", None, "tp"),
            P("shard", "tp"),
            P("rep", "shard", "tp"),
            P("shard", "rep", None, "tp"),
            P("shard", "tp"),
            P("rep", "shard", "tp"),
            P("shard", "rep", None, "tp"),
            P(("shard", "tp")),
            P(("shard", "tp")),
            P("shard", "tp"),
            P("shard", "rep", None, "tp"),
        ),
        check_vma=False,
    )
```

profile of v0, /device:TPU:1, one launch (start us, length us, event | category | flops | bytes accessed | tf_op | source)
XLA Modules:
  0.0 1561.7 jit_solution(1362675693380436460)
XLA Ops:
  8.1 1.3 fusion.11
  9.4 1.2 fusion.20
  11.9 61.7 %all-reduce.5 = (f32[32,32]{1,0:T(8,128)S(1)}, f32[32,32]{1,0:T(8,128)S(1)}, f32[128,32]{0,1:T(8,128)S(1)}) all-reduce(f32[32,32]{1,0:T(8,128)S(1)} %fusion.29, f32[32,32]{1,0:T(8,128)S(1)} %fusion.11, f32[128,32]{0,1:T(8,128)S(1)} %fusion.20), channel_id=1, replica_groups=mesh['rep'=4,'shard'=32,'tp'=4] {'rep','tp'}, use_global_device_ids=true, to_apply=%region_0.0 | all-reduce | flops 6144 | bytes 49152 | tf_op jit(solution)/shard_map/psum | solution.py:80
  74.1 107.7 %all-reduce.3 = (f32[32,32]{0,1:T(8,128)S(1)}, f32[32,32]{0,1:T(8,128)S(1)}, f32[32,32]{0,1:T(8,128)S(1)}) all-reduce(f32[32,32]{0,1:T(8,128)S(1)} %fusion.68, f32[32,32]{0,1:T(8,128)S(1)} %fusion.70, f32[32,32]{0,1:T(8,128)S(1)} %fusion.72), channel_id=1, replica_groups=mesh['rep'=4,'shard'=32,'tp'=4] {'shard'}, use_global_device_ids=true, to_apply=%region_1.0 | all-reduce | flops 3072 | bytes 24576 | tf_op jit(solution)/shard_map/psum | solution.py:82
  182.0 2.9 cholesky.126
  186.2 2.4 custom-call.15
  188.9 2.1 fusion.9
  191.0 2.9 cholesky.104
  195.3 2.4 custom-call.13
  198.0 1.8 fusion.27
  199.8 2.9 cholesky.148
  204.1 2.4 custom-call.17
  207.8 488.9 %psum.147 = f32[256,32]{0,1:T(8,128)S(1)} all-reduce(f32[256,32]{0,1:T(8,128)S(1)} %fusion.18), channel_id=1, replica_groups=mesh['rep'=4,'shard'=32,'tp'=4] {'rep','shard'}, use_global_device_ids=true, to_apply=%region_16.0 | all-reduce | flops 8192 | bytes 65536 | tf_op jit(solution)/shard_map/psum | solution.py:88
  699.1 1.4 fusion.7
  700.5 56.1 %all-reduce.4 = (f32[32,32]{1,0:T(8,128)S(1)}, f32[32,32]{1,0:T(8,128)S(1)}, f32[128,32]{0,1:T(8,128)S(1)}) all-reduce(f32[32,32]{1,0:T(8,128)S(1)} %fusion.25, f32[32,32]{1,0:T(8,128)S(1)} %fusion.7, f32[128,32]{0,1:T(8,128)S(1)} %fusion.16), channel_id=1, replica_groups=mesh['rep'=4,'shard'=32,'tp'=4] {'rep','tp'}, use_global_device_ids=true, to_apply=%region_5.8 | all-reduce | flops 6144 | bytes 49152 | tf_op jit(solution)/shard_map/psum | solution.py:80
  757.2 105.7 %all-reduce.2 = (f32[32,32]{0,1:T(8,128)S(1)}, f32[32,32]{0,1:T(8,128)S(1)}, f32[32,32]{0,1:T(8,128)S(1)}) all-reduce(f32[32,32]{0,1:T(8,128)S(1)} %fusion.69, f32[32,32]{0,1:T(8,128)S(1)} %fusion.71, f32[32,32]{0,1:T(8,128)S(1)} %fusion.73), channel_id=1, replica_groups=mesh['rep'=4,'shard'=32,'tp'=4] {'shard'}, use_global_device_ids=true, to_apply=%region_6.9 | all-reduce | flops 3072 | bytes 24576 | tf_op jit(solution)/shard_map/psum | solution.py:82
  862.9 2.9 cholesky.137
  867.2 2.4 custom-call.16
  869.9 2.1 fusion.5
  872.0 2.9 cholesky.115
  876.3 2.4 custom-call.14
  878.9 1.8 fusion.23
  881.5 73.9 %all_gather.21 = s32[1,16384]{1,0:T(1,128)S(1)} all-gather(s32[1,128]{1,0:T(1,128)} %param.47), channel_id=1, replica_groups=mesh['rep'=4,'shard'=32,'tp'=4] {'rep','shard'}, dimensions={1}, use_global_device_ids=true | all-gather | bytes 66048 | tf_op jit(solution)/shard_map/all_gather | solution.py:110
  957.4 9.0 psum.151
  967.6 2.9 cholesky.159
  971.9 2.4 custom-call.18
  975.7 487.8 %psum.150 = f32[256,32]{0,1:T(8,128)S(1)} all-reduce(f32[256,32]{0,1:T(8,128)S(1)} %fusion.14), channel_id=1, replica_groups=mesh['rep'=4,'shard'=32,'tp'=4] {'rep','shard'}, use_global_device_ids=true, to_apply=%region_19.23 | all-reduce | flops 8192 | bytes 65536 | tf_op jit(solution)/shard_map/psum | solution.py:88
  1463.8 1.4 fusion.66
  1465.2 9.1 all-gather.2
  1474.3 1.6 fusion.22
  1475.8 1.4 convolution_multiply_fusion
  1477.9 9.4 all-gather.1
  1489.1 9.3 all-gather
  1499.8 40.2 %while.11 = (s32[]{:T(128)}, f32[250,256]{1,0:T(8,128)S(1)}, s32[32,512]{1,0:T(8,128)S(1)}, s32[]{:T(128)}, bf16[32,512,256]{2,1,0:T(8,128)(2,1)}, /*index=5*/s32[]{:T(128)}, s32[]{:T(128)}) while((s32[]{:T(128)}, f32[250,256]{1,0:T(8,128)S(1)}, s32[32,512]{1,0:T(8,128)S(1)}, s32[]{:T(128)}, bf16[32,512,256]{2,1,0:T(8,128)(2,1)}, ...), condition=%wide.region_22.26_spmd.clone, body=%wide.region_21.25_spmd.clone.sunk | while | flops 65792512 | bytes 780895 | solution.py:39
  1499.9 1.2 convolution_add_fusion.2
  1501.1 1.2 convolution_add_fusion.2
  1502.4 1.2 convolution_add_fusion.2
  1503.6 1.2 convolution_add_fusion.2
  1504.9 1.2 convolution_add_fusion.2
  1506.1 1.2 convolution_add_fusion.2
  1507.4 1.2 convolution_add_fusion.2
  1508.7 1.2 convolution_add_fusion.2
  1509.9 1.2 convolution_add_fusion.2
  1511.2 1.2 convolution_add_fusion.2
  1512.4 1.2 convolution_add_fusion.2
  1513.7 1.2 convolution_add_fusion.2
  1514.9 1.2 convolution_add_fusion.2
  1516.2 1.2 convolution_add_fusion.2
  1517.5 1.2 convolution_add_fusion.2
  1518.7 1.2 convolution_add_fusion.2
  1520.0 1.2 convolution_add_fusion.2
  1521.2 1.2 convolution_add_fusion.2
  1522.5 1.2 convolution_add_fusion.2
  1523.7 1.2 convolution_add_fusion.2
  1525.0 1.2 convolution_add_fusion.2
  1526.3 1.2 convolution_add_fusion.2
  1527.5 1.2 convolution_add_fusion.2
  1528.8 1.2 convolution_add_fusion.2
  1530.0 1.2 convolution_add_fusion.2
  1531.3 1.2 convolution_add_fusion.2
  1533.8 1.2 convolution_add_fusion.2
  1535.1 1.2 convolution_add_fusion.2
  1538.8 1.2 convolution_add_fusion.2
  1540.2 11.0 all-gather.4
  (130 shorter events, 33.9 us)
Async XLA Ops:
  7.2 1.0 copy-start
  7.2 1491.9 %copy-start.2 = (bf16[1,32,2048]{2,1,0:T(8,128)(2,1)S(1)}, bf16[1,32,2048]{2,1,0:T(8,128)(2,1)}, u32[]{:S(2)}) copy-start(bf16[1,32,2048]{2,1,0:T(8,128)(2,1)} %param.34) | copy-start | bytes 393220
  7.2 1491.9 %copy-start.1 = (f32[1,32,2048]{2,1,0:T(8,128)S(1)}, f32[1,32,2048]{2,1,0:T(8,128)}, u32[]{:S(2)}) copy-start(f32[1,32,2048]{2,1,0:T(8,128)} %param.35) | copy-start | bytes 786436
  7.2 1491.2 %copy-start.4 = (bf16[1,32,768]{2,1,0:T(8,128)(2,1)S(1)}, bf16[1,32,768]{2,1,0:T(8,128)(2,1)}, u32[]{:S(2)}) copy-start(bf16[1,32,768]{2,1,0:T(8,128)(2,1)} %param.29) | copy-start | bytes 147460
  7.2 1491.2 %copy-start.3 = (f32[1,32,768]{2,1,0:T(8,128)S(1)}, f32[1,32,768]{2,1,0:T(8,128)}, u32[]{:S(2)}) copy-start(f32[1,32,768]{2,1,0:T(8,128)} %param.30) | copy-start | bytes 294916
  7.2 1470.0 %copy-start.8 = (f32[1,1,8,2048]{3,2,1,0:T(8,128)S(1)}, f32[1,1,8,2048]{3,2,1,0:T(8,128)}, u32[]{:S(2)}) copy-start(f32[1,1,8,2048]{3,2,1,0:T(8,128)} %param.37) | copy-start | bytes 196612
  7.3 1470.0 %copy-start.7 = (f32[1,1,8,2048]{3,2,1,0:T(8,128)S(1)}, f32[1,1,8,2048]{3,2,1,0:T(8,128)}, u32[]{:S(2)}) copy-start(f32[1,1,8,2048]{3,2,1,0:T(8,128)} %param.38) | copy-start | bytes 196612
  7.3 1481.2 %copy-start.10 = (f32[1,1,8,768]{3,2,1,0:T(8,128)S(1)}, f32[1,1,8,768]{3,2,1,0:T(8,128)}, u32[]{:S(2)}) copy-start(f32[1,1,8,768]{3,2,1,0:T(8,128)} %param.32) | copy-start | bytes 73732
  7.3 1481.2 %copy-start.9 = (f32[1,1,8,768]{3,2,1,0:T(8,128)S(1)}, f32[1,1,8,768]{3,2,1,0:T(8,128)}, u32[]{:S(2)}) copy-start(f32[1,1,8,768]{3,2,1,0:T(8,128)} %param.33) | copy-start | bytes 73732
  7.3 1532.8 %copy-start.6 = (f32[1,1,250,256]{3,1,2,0:T(1,128)S(1)}, f32[1,1,250,256]{3,1,2,0:T(1,128)}, u32[]{:S(2)}) copy-start(f32[1,1,250,256]{3,1,2,0:T(1,128)} %param.49) | copy-start | bytes 768004
  7.3 1532.8 %copy-start.5 = (f32[1,1,250,256]{3,1,2,0:T(1,128)S(1)}, f32[1,1,250,256]{3,1,2,0:T(1,128)}, u32[]{:S(2)}) copy-start(f32[1,1,250,256]{3,1,2,0:T(1,128)} %param.50) | copy-start | bytes 768004
  7.3 690.6 %all-reduce.11.cloned.1.call-start = ((), (), s32[]{:S(2)}) async-start(), calls=%async_computation.2 | async-start | bytes 720896 | tf_op jit(solution)/shard_map/psum | solution.py:88
  199.8 1276.1 %all-reduce.9.cloned.1.call-start = ((), (), s32[]{:S(2)}) async-start(), calls=%async_computation.1 | async-start | bytes 720896 | tf_op jit(solution)/shard_map/psum | solution.py:88
  880.7 619.1 %all-gather.7.cloned.1.call-start = ((), (), s32[]{:S(2)}) async-start(), calls=%async_computation | async-start | bytes 8454144 | tf_op jit(solution)/shard_map/all_gather | solution.py:111
Sparse Core Ops, SparseCore 0:
  199.9 327.1 all-reduce.10
  880.9 320.3 all-reduce.8
  1204.4 144.7 all-gather.6
where the time goes:
time: 1580 us; the launch traced here: 1560 us
  blocking collectives  1430 us (91%)
  matrix products  61.4 us (4%)
  other arithmetic  49 us (3%)
    psum x2, blocking collectives, on_device(): lax.psum((raw_rights[0], raw_rights[1], raw_rights[2]), ('rep', 'shard'))  977 us
    psum x2, blocking collectives, on_device(): summed = lax.psum((grams[0], grams[1], grams[2]), 'shard')  213 us
    psum x2, blocking collectives, on_device(): lefts = [lax.psum(left_part, ('rep', 'tp')) for left_part in parts]  118 us
    all_gather x1, blocking collectives, on_device(): lax.all_gather(emb_ids, ('rep', 'shard'), axis=1, tiled=True)  73.9 us
    dot_general x32, matrix products, one_block(): jnp.dot(one_hot, block_values, preferred_element_type=jnp.float32)  38.6 us
  transfers between devices with their start and end apart: 3, of which 0 were waited for; matrix products, arithmetic and copies ran while one was open for 2% of the time, Pallas kernels for 0%

commit v1 on v0

v1 whole, which is shorter than its diff:
```python
import jax
import jax.numpy as jnp
from jax import lax
from jax.experimental import pallas as pl
from jax.experimental.pallas import tpu as pltpu
from jax.sharding import PartitionSpec as P

ROUNDS = 2
RANK = 32
GRAM_CHUNK = 24

momentum_decay = 0.9
step_size = 0.05

MESH = pl.DeviceIdType.MESH
HIGH = lax.Precision.HIGHEST


def dot_nn(a, b):
    return lax.dot_general(a, b, (((1,), (0,)), ((), ())), precision=HIGH, preferred_element_type=jnp.float32)


def dot_nt(a, b):
    return lax.dot_general(a, b, (((1,), (1,)), ((), ())), precision=HIGH, preferred_element_type=jnp.float32)


def inverse_factors(grams):
    row = lax.broadcasted_iota(jnp.int32, (RANK, 128), 0)
    lane = lax.broadcasted_iota(jnp.int32, (RANK, 128), 1)
    lefts = list(grams)
    rights = [jnp.where(row == lane, 1.0, 0.0).astype(jnp.float32) for _ in grams]
    for j in range(RANK):
        for m in range(len(lefts)):
            a, e = lefts[m], rights[m]
            pivot = a[j : j + 1, j : j + 1]
            scale = lax.rsqrt(pivot)
            scale = scale * (1.5 - 0.5 * (pivot * scale) * scale)
            row_a = a[j : j + 1, :] * scale
            row_e = e[j : j + 1, :] * scale
            column = a[:, j : j + 1] * scale
            lefts[m] = jnp.where(row > j, a - column * row_a, a)
            rights[m] = jnp.where(row > j, e - column * row_e, jnp.where(row == j, row_e, e))
    return [e[:, :RANK] for e in rights]


def sgd_kernel(rows, cols, *refs):
    (
        qg, qe, qb, gg, ge, gb, dg, de, db, uq, ug, ud, vec,
        approx_q, approx_g, approx_d, gath_q, gath_g, gath_d, vec_sum,
        full_q, full_g, full_d, basis, land_q, land_g, land_d, land_v,
        xbuf, ybuf, wide, half, from_core, from_y, mine, from_z, whole,
        u_send, u_recv, x_send, x_recv, y_send, y_recv, c_send, c_recv,
        ry_send, ry_recv, rz_send, rz_recv, gz_send, gz_recv, gy_send, gy_recv, gc_send, gc_recv,
    ) = refs
    y = lax.axis_index("rep")
    s = lax.axis_index("shard")
    x = lax.axis_index("tp")
    z = s // 2
    core = s % 2
    other = 1 - core

    def at_x(d):
        return (y, s, (x + d) % 4)

    def at_y(d):
        return ((y + d) % 4, s, x)

    def at_z(d):
        return (y, ((z + d) % 16) * 2 + core, x)

    partner = (y, z * 2 + other, x)
    barrier = pltpu.get_barrier_semaphore()
    peers = [at_x(d) for d in (1, 2, 3)] + [at_y(d) for d in (1, 2, 3)]
    peers += [at_z(d) for d in range(1, 16)] + [partner]
    for peer in peers:
        pl.semaphore_signal(barrier, inc=1, device_id=peer, device_id_type=MESH)

    fulls = (full_q, full_g, full_d)
    for full, g, e in zip(fulls, (qg, gg, dg), (qe, ge, de)):
        full[...] = g[0].astype(jnp.float32) + e[0]
    starts = (0, cols[0], cols[0] + cols[1])
    for m, b in enumerate((qb, gb, db)):
        basis[:, starts[m] : starts[m] + cols[m]] = b[...]
    for r in range(ROUNDS):
        xbuf[r, x] = jnp.zeros(xbuf.shape[2:], jnp.float32)
        for c in range(GRAM_CHUNK, 32):
            wide[r, :, c] = jnp.zeros((4, 8, 128), jnp.float32)
    pl.semaphore_wait(barrier, len(peers))

    def copy(src, dst, send, recv, device):
        made = pltpu.make_async_remote_copy(
            src_ref=src, dst_ref=dst, send_sem=send, recv_sem=recv, device_id=device, device_id_type=MESH
        )
        made.start()
        return made

    early = []
    for k, (src, land) in enumerate(((uq, land_q), (ug, land_g), (ud, land_d), (vec, land_v))):
        for d in (1, 2, 3):
            early.append(copy(src, land.at[y], u_send.at[k, d], u_recv.at[k, d], at_y(d)))

    def finish(copies):
        for made in copies:
            made.wait_send()
            made.wait_recv()

    for r in range(ROUNDS):
        for m in range(3):
            part = dot_nt(basis[:, starts[m] : starts[m] + cols[m]], fulls[m][...])
            xbuf[r, x, m, :, : rows[m]] = part
        finish([copy(xbuf.at[r, x], xbuf.at[r, x], x_send.at[r, d], x_recv.at[r, d], at_x(d)) for d in (1, 2, 3)])
        ybuf[r, y] = (xbuf[r, 0] + xbuf[r, 1]) + (xbuf[r, 2] + xbuf[r, 3])
        finish([copy(ybuf.at[r, y], ybuf.at[r, y], y_send.at[r, d], y_recv.at[r, d], at_y(d)) for d in (1, 2, 3)])
        left = (ybuf[r, 0] + ybuf[r, 1]) + (ybuf[r, 2] + ybuf[r, 3])
        for m in range(3):
            raw = dot_nn(left[m][:, : rows[m]], fulls[m][...])
            for c in range(cols[m] // 128):
                wide[r, :, starts[m] // 128 + c] = raw[:, c * 128 : (c + 1) * 128].reshape(4, 8, 128)
            gram = dot_nt(left[m], left[m]) * 0.25
            wide[r, :, GRAM_CHUNK + m, :, :RANK] = gram.reshape(4, 8, RANK)
        finish([copy(wide.at[r, :, pl.ds(other * 16, 16)], from_core.at[r], c_send.at[r], c_recv.at[r], partner)])
        half[r] = wide[r, :, pl.ds(core * 16, 16)] + from_core[r]
        finish([
            copy(half.at[r, (y + d) % 4], from_y.at[r, d - 1], ry_send.at[r, d], ry_recv.at[r, d], at_y(d))
            for d in (1, 2, 3)
        ])
        mine[r] = (half[r, y] + from_y[r, 0]) + (from_y[r, 1] + from_y[r, 2])
        finish([
            copy(mine.at[r, (z + d) % 16], from_z.at[r, d - 1], rz_send.at[r, d], rz_recv.at[r, d], at_z(d))
            for d in range(1, 16)
        ])
        tiles = [mine[r, z]] + [from_z[r, k] for k in range(15)]
        while len(tiles) > 1:
            tiles = [tiles[k] + tiles[k + 1] for k in range(0, len(tiles), 2)]
        whole[r, core, y, z] = tiles[0]
        spot = whole.at[r, core, y, z]
        finish([copy(spot, spot, gz_send.at[r, d], gz_recv.at[r, d], at_z(d)) for d in range(1, 16)])
        spot_y = whole.at[r, core, y]
        finish([copy(spot_y, spot_y, gy_send.at[r, d], gy_recv.at[r, d], at_y(d)) for d in (1, 2, 3)])
        spot_c = whole.at[r, core]
        finish([copy(spot_c, spot_c, gc_send.at[r], gc_recv.at[r], partner)])
        grams = [whole[r, 1, :, GRAM_CHUNK - 16 + m].reshape(RANK, 128) for m in range(3)]
        inverses = inverse_factors(grams)
        for m in range(3):
            first = starts[m] // 128
            chunks = [
                whole[r, c // 16, :, c % 16].reshape(RANK, 128) for c in range(first, first + cols[m] // 128)
            ]
            basis[:, starts[m] : starts[m] + cols[m]] = dot_nn(inverses[m], jnp.concatenate(chunks, axis=1))
    for m, approx in enumerate((approx_q, approx_g, approx_d)):
        ortho = dot_nn(inverses[m], left[m])
        ortho = ortho.T[: rows[m], :]
        approx[...] = dot_nn(ortho, basis[:, starts[m] : starts[m] + cols[m]]) * 0.25
    finish(early)
    for src, land in ((uq, land_q), (ug, land_g), (ud, land_d), (vec, land_v)):
        land[y] = src[...]
    gath_q[...] = land_q[...]
    gath_g[...] = land_g[...]
    gath_d[...] = land_d[...]
    vec_sum[...] = (land_v[0] + land_v[1]) + (land_v[2] + land_v[3])


def power_sgd(grads, errors, bases, updates, vec_tile):
    rows = tuple(g.shape[1] for g in grads)
    cols = tuple(g.shape[2] for g in grads)
    operands = []
    for g, e, b in zip(grads, errors, bases):
        operands += [g, e, b]
    operands += list(updates) + [vec_tile]
    f32 = jnp.float32
    out_shape = [jax.ShapeDtypeStruct((rows[m], cols[m]), f32) for m in range(3)]
    out_shape += [jax.ShapeDtypeStruct((4,) + u.shape, f32) for u in updates]
    out_shape += [jax.ShapeDtypeStruct((8, 128), f32)]
    dma = pltpu.SemaphoreType.DMA
    scratch = [pltpu.VMEM((rows[m], cols[m]), f32) for m in range(3)]
    scratch += [pltpu.VMEM((RANK, sum(cols)), f32)]
    scratch += [pltpu.VMEM((4,) + u.shape, f32) for u in updates]
    scratch += [
        pltpu.VMEM((4, 8, 128), f32),
        pltpu.VMEM((ROUNDS, 4, 3, RANK, 128), f32),
        pltpu.VMEM((ROUNDS, 4, 3, RANK, 128), f32),
        pltpu.VMEM((ROUNDS, 4, 32, 8, 128), f32),
        pltpu.VMEM((ROUNDS, 4, 16, 8, 128), f32),
        pltpu.VMEM((ROUNDS, 4, 16, 8, 128), f32),
        pltpu.VMEM((ROUNDS, 3, 16, 8, 128), f32),
        pltpu.VMEM((ROUNDS, 16, 8, 128), f32),
        pltpu.VMEM((ROUNDS, 15, 8, 128), f32),
        pltpu.VMEM((ROUNDS, 2, 4, 16, 8, 128), f32),
    ]
    for shape in ((4, 4), (ROUNDS, 4), (ROUNDS, 4), (ROUNDS,), (ROUNDS, 4), (ROUNDS, 16), (ROUNDS, 16), (ROUNDS, 4), (ROUNDS,)):
        scratch += [dma(shape), dma(shape)]
    vmem = pl.BlockSpec(memory_space=pltpu.VMEM)

    def body(*refs):
        sgd_kernel(rows, cols, *refs)

    return pl.pallas_call(
        body,
        out_shape=out_shape,
        in_specs=[vmem] * len(operands),
        out_specs=[vmem] * len(out_shape),
        scratch_shapes=scratch,
        compiler_params=pltpu.CompilerParams(collective_id=0, has_side_effects=True, vmem_limit_bytes=24 * 1024 * 1024),
        cost_estimate=pl.CostEstimate(flops=400_000_000, bytes_accessed=400_000_000, transcendentals=0),
        name="power_sgd",
    )(*operands)


def add_rows(ids, values, block_rows):
    groups, stacked, _, width = values.shape[0], 8, values.shape[1], values.shape[2]
    per = ids.shape[1]
    padded = (block_rows + 15) // 16 * 16

    def body(ids_ref, values_ref, out_ref):
        @pl.when(pl.program_id(0) == 0)
        def _():
            out_ref[...] = jnp.zeros_like(out_ref)

        spots = lax.broadcasted_iota(jnp.int32, (padded, stacked * per), 0)
        one_hot = jnp.where(spots == ids_ref[0], 1.0, 0.0).astype(jnp.bfloat16)
        block = values_ref[:, :per, :].reshape(stacked * per, width)
        out_ref[...] += jnp.dot(one_hot, block, preferred_element_type=jnp.float32)

    return pl.pallas_call(
        body,
        grid=(groups // stacked,),
        in_specs=[
            pl.BlockSpec((1, 1, stacked * per), lambda k: (k, 0, 0)),
            pl.BlockSpec((stacked, values.shape[1], width), lambda k: (k, 0, 0)),
        ],
        out_specs=pl.BlockSpec((padded, width), lambda k: (0, 0)),
        out_shape=jax.ShapeDtypeStruct((padded, width), jnp.float32),
        name="add_rows",
    )(ids.reshape(groups // stacked, 1, stacked * per), values)[:block_rows]


def on_device(
    qkv_grad, qkv_error, qkv_basis, qkv_weight, qkv_moment,
    gu_grad, gu_error, gu_basis, gu_weight, gu_moment,
    down_grad, down_error, down_basis, down_weight, down_moment,
    vec_grad, vec_weight, vec_moment,
    emb_ids, emb_grad, emb_weight, emb_moment,
):
    rep_count = lax.axis_size("rep")
    rep_index = lax.axis_index("rep")
    shard_index = lax.axis_index("shard")
    low = (emb_ids[0] % 256).astype(jnp.bfloat16)
    top = (emb_ids[0] // 256).astype(jnp.bfloat16)
    per = emb_ids.shape[1]
    extra = jnp.concatenate([low, top]).reshape(1, 2 * per)
    sent = jnp.concatenate([emb_grad[0], extra, jnp.zeros((15, 2 * per), jnp.bfloat16)], axis=0)
    gathered = lax.all_gather(sent, ("rep", "shard"), axis=0, tiled=True)
    gathered = gathered.reshape(-1, sent.shape[0], sent.shape[1])

    weights = (qkv_weight[0, 0], gu_weight[0, 0], down_weight[0, 0])
    moments = (qkv_moment[0, 0], gu_moment[0, 0], down_moment[0, 0])
    updates = [w - (step_size * momentum_decay) * m for w, m in zip(weights, moments)]
    vec_len = vec_weight.shape[0]
    vec_tile = jnp.pad(vec_grad.astype(jnp.float32), ((0, 7), (0, 128 - vec_len)))
    outs = power_sgd(
        (qkv_grad, gu_grad, down_grad),
        (qkv_error, gu_error, down_error),
        (qkv_basis.T, gu_basis.T, down_basis.T),
        updates,
        vec_tile,
    )
    approxes, olds, vec_sum = outs[:3], outs[3:6], outs[6]
    results = []
    for index, (grad, error) in enumerate(((qkv_grad, qkv_error), (gu_grad, gu_error), (down_grad, down_error))):
        approx = approxes[index]
        error_new = (grad[0].astype(jnp.float32) + error[0] - approx)[None]
        local_rows = weights[index].shape[0]
        own_rows = lax.dynamic_slice_in_dim(approx, rep_index * local_rows, local_rows, 0)
        moment_new = (momentum_decay * moments[index] + own_rows)[None, None]
        plain = olds[index].reshape(approx.shape) - step_size * approx
        results += [plain, error_new, moment_new]
    vec_mean = vec_sum[0, :vec_len] / rep_count
    vec_moment_new = momentum_decay * vec_moment + vec_mean
    vec_new = vec_weight - step_size * vec_moment_new

    block_rows = emb_weight.shape[2]
    row_start = (shard_index * rep_count + rep_index) * block_rows
    digits = gathered[:, per, :].astype(jnp.int32)
    row_ids = digits[:, :per] + 256 * digits[:, per:] - row_start
    emb_sum = add_rows(row_ids, gathered, block_rows) / rep_count
    emb_moment_new = momentum_decay * emb_moment[0, 0] + emb_sum
    emb_flat_new = (emb_weight[0, 0] - step_size * emb_moment_new)[None, None]
    emb_whole = lax.all_gather(emb_flat_new, "rep", axis=1, tiled=True)
    emb_new = emb_whole.reshape(emb_whole.shape[1] * emb_whole.shape[2], emb_whole.shape[3])
    return (*results, vec_new, vec_moment_new, emb_new, emb_moment_new[None, None])


def solution(mesh):
    grouped = P("shard", "rep", None, "tp")
    matrix = P("rep", "shard", "tp")
    per_matrix = (matrix, matrix, P("tp", None), grouped, grouped)
    vector = P(("shard", "tp"))
    return jax.shard_map(
        on_device,
        mesh=mesh,
        in_specs=per_matrix * 3
        + (P("rep", ("shard", "tp")), vector, vector, P("rep", "shard"), matrix, grouped, grouped),
        out_specs=(P("shard", "tp"), matrix, grouped) * 3 + (vector, vector, P("shard", "tp"), grouped),
        check_vma=False,
    )
```

time: 1580 us -> 209 us (0.13)
  blocking collectives: 1430 us -> 12.5 us
  Pallas kernels: 0 us -> 123 us
  matrix products: 61.4 us -> 0 us
  other arithmetic: 49 us -> 15.9 us
  waiting for transfers between devices: 0.74 us -> 29.5 us
    psum x7 -> x0, blocking collectives: 1320 us -> none  [the longest x2 977 us: on_device(): lax.psum((raw_rights[0], raw_rights[1], raw_rights[2]), ('rep', 'shard'))]
    pallas_call x0 -> x2, Pallas kernels: none -> 123 us  [the longest x1 110 us: power_sgd(): pl.pallas_call(body, out_shape=out_shape, in_specs=[vmem] * len(operands)...]
    all_gather x5 -> x1, blocking collectives: 113 us -> 12.5 us  [on_device(): emb_whole = lax.all_gather(emb_flat_new, 'rep', axis=1, tiled=True)]
    dot_general x53 -> x0, matrix products: 60 us -> none  [the longest x32 38.6 us: one_block(): jnp.dot(one_hot, block_values, preferred_element_type=jnp.float32)]
    another operation x30 -> x0, other arithmetic: 40.1 us -> none  [the longest x18 21.6 us: on_device(): lowers = [jnp.linalg.cholesky(summed[index]) for index in range(3)]]
    all_gather x1, waiting for transfers between devices: 0.01 us -> 29.5 us  [on_device(): gathered = lax.all_gather(sent, ('rep', 'shard'), axis=0, tiled=True)]
  transfers between devices with their start and end apart: 3 -> 1, of which waited for: 0 -> 1; matrix products, arithmetic and copies ran while one was open for 2% -> 5% of each run, Pallas kernels for 0% -> 54%
where the time goes in v1:
time: 209 us; the launch traced here: 205 us
  Pallas kernels  123 us (59%)
  waiting for transfers between devices  29.5 us (14%)
  other arithmetic  15.9 us (8%)
  between operations  14.1 us (7%)
  blocking collectives  12.5 us (6%)
  local copies, waits for them, and re-layouts  10 us (5%)
    pallas_call x1, Pallas kernels, power_sgd(): pl.pallas_call(body, out_shape=out_shape, in_specs=[vmem] * len(operands)...  110 us
    all_gather x1, waiting for transfers between devices, on_device(): gathered = lax.all_gather(sent, ('rep', 'shard'), axis=0, tiled=True)  29.5 us
    all_gather x1, blocking collectives, on_device(): emb_whole = lax.all_gather(emb_flat_new, 'rep', axis=1, tiled=True)  12.5 us
    pallas_call x1, Pallas kernels, add_rows(): pl.pallas_call(body, grid=(groups // stacked,), in_specs=[pl.BlockSpec((1...  12.5 us
    unnamed x25, local copies, waits for them, and re-layouts  9.94 us
    broadcast_in_dim x3, other arithmetic, on_device(): moment_new = (momentum_decay * moments[index] + own_rows)[None, None]  4.2 us
  transfers between devices with their start and end apart: 1, of which 1 were waited for; matrix products, arithmetic and copies ran while one was open for 5% of the time, Pallas kernels for 54%

profile of v1, /device:TPU:1, one launch (start us, length us, event | category | flops | bytes accessed | tf_op | source)
XLA Modules:
  0.0 205.0 jit_solution(9684325889831186260)
XLA Ops:
  7.2 0.0 copy-start.9
  7.2 0.0 copy-start.10
  7.2 0.0 all-gather.4.cloned.1.call-start
  7.2 0.8 fusion.11
  8.0 0.1 pad.10.clone
  8.1 1.6 maximum_maximum_fusion
  9.7 0.0 all-gather.4.cloned.1.call-update
  9.7 0.7 pad_convert_fusion.refs_12_
  10.4 0.8 subtract_bitcast_fusion.2.refs_9_
  11.1 0.8 subtract_bitcast_fusion.1.refs_11_
  11.9 0.9 subtract_bitcast_fusion.refs_10_
  12.8 0.0 copy-start
  12.8 0.9 copy-done
  13.7 0.0 copy-start.1
  13.7 0.9 copy-done.1
  14.6 0.0 copy-start.2
  14.7 0.9 copy-done.2
  15.6 0.0 copy-start.3
  15.6 0.9 copy-done.3
  16.4 0.0 copy-start.4
  16.4 0.8 copy-done.4
  17.3 0.0 copy-start.5
  17.3 0.8 copy-done.5
  18.1 0.0 copy-start.6
  18.1 0.9 copy-done.6
  19.0 0.0 copy-start.7
  19.0 0.9 copy-done.7
  19.9 0.0 copy-start.8
  19.9 0.8 copy-done.8
  20.7 110.5 %power_sgd.1 = (f32[32,768]{1,0:T(8,128)S(1)}, f32[32,2048]{1,0:T(8,128)S(1)}, f32[128,256]{1,0:T(8,128)S(1)}, f32[4,8,768]{2,1,0:T(8,128)S(1)}, f32[4,8,2048]{2...) custom-call(bf16[1,32,768]{2,1,0:T(8,128)(2,1)S(1)} %copy-done.5, f32[1,32,768]{2,1,0:T(8,128)S(1)} %copy-done.3, ...), custom_call_target="tpu_custom_call" | custom-call | flops 400000000 | bytes 400000000 | tf_op jit(solution)/shard_map/power_sgd/pallas_call | solution.py:197
  131.2 1.2 multiply_subtract_fusion
  132.4 1.3 fusion.10
  133.7 1.4 fusion.9
  135.1 0.7 fusion.4
  135.8 0.7 fusion.3
  136.5 1.5 fusion.7
  138.0 0.8 fusion.2
  138.9 29.5 %all-gather.4.cloned.1.call-done = bf16[18432,256]{1,0:T(8,128)(2,1)} async-done(((bf16[144,256]{1,0:T(8,128)(2,1)}), bf16[18432,256]{1,0:T(8,128)(2,1)}) %all-gather.4.cloned.1.call-update) | async-done | bytes 9437200 | tf_op jit(solution)/shard_map/all_gather | solution.py:252
  168.3 1.1 slice_convert_fusion
  169.5 0.6 fusion.6
  170.1 12.5 %add_rows.1 = f32[256,256]{1,0:T(8,128)} custom-call(s32[16,1,1024]{2,1,0:T(1,128)} %bitcast.97, bf16[128,144,256]{2,1,0:T(8,128)(2,1)} %bitcast.95), custom_call_target="tpu_custom_call" | custom-call | tf_op jit(solution)/shard_map/add_rows/pallas_call | solution.py:224
  182.6 0.0 copy-done.9
  182.6 0.0 copy-done.10
  182.6 1.0 fusion.8
  183.7 1.0 copy.43
  184.6 12.5 %all-gather.1 = f32[4,250,256]{2,1,0:T(8,128)S(1)} all-gather(f32[1,250,256]{2,1,0:T(8,128)S(1)} %get-tuple-element.69), channel_id=2, replica_groups=mesh['rep'=4,'shard'=32,'tp'=4] {'rep'}, dimensions={0}, use_global_device_ids=true | all-gather | bytes 1280000 | tf_op jit(solution)/shard_map/all_gather | solution.py:288
  197.1 1.1 reshape.85
  (4 shorter events, 0.0 us)
Async XLA Ops:
  7.2 175.4 %copy-start.9 = (f32[1,1,250,256]{3,1,2,0:T(1,128)S(1)}, f32[1,1,250,256]{3,1,2,0:T(1,128)}, u32[]{:S(2)}) copy-start(f32[1,1,250,256]{3,1,2,0:T(1,128)} %param.43) | copy-start | bytes 768004
  7.2 175.4 %copy-start.10 = (f32[1,1,250,256]{3,1,2,0:T(1,128)S(1)}, f32[1,1,250,256]{3,1,2,0:T(1,128)}, u32[]{:S(2)}) copy-start(f32[1,1,250,256]{3,1,2,0:T(1,128)} %param.42) | copy-start | bytes 768004
  7.2 161.1 %all-gather.4.cloned.1.call-start = ((), (), s32[]{:S(2)}) async-start(), calls=%async_computation | async-start | bytes 9510912 | tf_op jit(solution)/shard_map/all_gather | solution.py:252
  12.8 1.0 copy-start
  13.7 0.9 copy-start.1
  14.6 0.9 copy-start.2
  15.6 0.9 copy-start.3
  16.4 0.8 copy-start.4
  17.3 0.8 copy-start.5
  18.1 0.9 copy-start.6
  19.0 0.9 copy-start.7
  19.9 0.8 copy-start.8
Sparse Core Ops, SparseCore 0:
  11.7 156.5 all-gather.3

commit v2 on v1

v2 whole, which is shorter than its diff:
```python
import jax
import jax.numpy as jnp
from jax import lax
from jax.experimental import pallas as pl
from jax.experimental.pallas import tpu as pltpu
from jax.sharding import PartitionSpec as P

ROUNDS = 2
RANK = 32
GRAM_CHUNK = 24

momentum_decay = 0.9
step_size = 0.05

MESH = pl.DeviceIdType.MESH
HIGH = lax.Precision.HIGHEST


def dot_nn(a, b):
    return lax.dot_general(a, b, (((1,), (0,)), ((), ())), precision=HIGH, preferred_element_type=jnp.float32)


def dot_nt(a, b):
    return lax.dot_general(a, b, (((1,), (1,)), ((), ())), precision=HIGH, preferred_element_type=jnp.float32)


def inverse_factors(grams):
    row = lax.broadcasted_iota(jnp.int32, (RANK, 128), 0)
    lane = lax.broadcasted_iota(jnp.int32, (RANK, 128), 1)
    lefts = list(grams)
    rights = [jnp.where(row == lane, 1.0, 0.0).astype(jnp.float32) for _ in grams]
    for j in range(RANK):
        for m in range(len(lefts)):
            a, e = lefts[m], rights[m]
            pivot = a[j : j + 1, j : j + 1]
            scale = lax.rsqrt(pivot)
            scale = scale * (1.5 - 0.5 * (pivot * scale) * scale)
            row_a = a[j : j + 1, :] * scale
            row_e = e[j : j + 1, :] * scale
            column = a[:, j : j + 1] * scale
            lefts[m] = jnp.where(row > j, a - column * row_a, a)
            rights[m] = jnp.where(row > j, e - column * row_e, jnp.where(row == j, row_e, e))
    return [e[:, :RANK] for e in rights]


def sgd_kernel(rows, cols, block_rows, *refs):
    (
        qg_hbm, qe_hbm, qb_hbm, qw_hbm, qm_hbm, gg_hbm, ge_hbm, gb_hbm, gw_hbm, gm_hbm,
        dg_hbm, de_hbm, db_hbm, dw_hbm, dm_hbm, rows_hbm, ew_hbm, em_hbm, ids, vec,
        approx_q, approx_g, approx_d, gath_q, gath_g, gath_d, vec_sum, emb_out, emb_moment_out,
        qg, qe, qb, qw, qm, gg, ge, gb, gw, gm, dg, de, db, dw, dm, ew, em,
        full_q, full_g, full_d, basis, land_q, land_g, land_d, land_v,
        xbuf, ybuf, wide, half, from_core, from_y, mine, from_z, whole,
        blocks, id_rows, part_own, part_send, part_land, emb_land,
        l_sem,
        u_send, u_recv, x_send, x_recv, y_send, y_recv, c_send, c_recv,
        ry_send, ry_recv, rz_send, rz_recv, gz_send, gz_recv, gy_send, gy_recv, gc_send, gc_recv,
        er_send, er_recv, el_send, el_recv, ec_send, ec_recv, p_send, p_recv, e_send, e_recv,
    ) = refs
    f32 = jnp.float32
    y = lax.axis_index("rep")
    s = lax.axis_index("shard")
    x = lax.axis_index("tp")
    z = s // 2
    core = s % 2
    other = 1 - core
    per = rows_hbm.shape[1]

    def at_x(d):
        return (y, s, (x + d) % 4)

    def at_y(d):
        return ((y + d) % 4, s, x)

    def at_z(d):
        return (y, ((z + d) % 16) * 2 + core, x)

    def block_at(d):
        return core * 16 + (z + d + 16) % 16

    partner = (y, z * 2 + other, x)
    barrier = pltpu.get_barrier_semaphore()
    peers = [at_x(d) for d in (1, 2, 3)] + [at_y(d) for d in (1, 2, 3)]
    peers += [at_z(d) for d in range(1, 16)] + [partner]
    for peer in peers:
        pl.semaphore_signal(barrier, inc=1, device_id=peer, device_id_type=MESH)

    own_block = blocks.at[core * 16 + z]
    pairs = [(rows_hbm.at[0], own_block.at[pl.ds(0, per)])]
    pairs += list(zip(
        (qg_hbm, qe_hbm, qb_hbm, gg_hbm, ge_hbm, gb_hbm, dg_hbm, de_hbm, db_hbm,
         qw_hbm, qm_hbm, gw_hbm, gm_hbm, dw_hbm, dm_hbm, ew_hbm, em_hbm),
        (qg, qe, qb, gg, ge, gb, dg, de, db, qw, qm, gw, gm, dw, dm, ew, em),
    ))
    local = [pltpu.make_async_copy(src, dst, l_sem.at[k]) for k, (src, dst) in enumerate(pairs)]
    for made in local:
        made.start()
    digits = jnp.broadcast_to(ids[...], (16, per))
    digits = jnp.concatenate([digits & 255, digits >> 8], axis=1).astype(f32).astype(jnp.bfloat16)
    blocks[core * 16 + z, per : per + 16, :] = digits
    for r in range(ROUNDS):
        xbuf[r, x] = jnp.zeros(xbuf.shape[2:], f32)
        for c in range(GRAM_CHUNK, 32):
            wide[r, :, c] = jnp.zeros((4, 8, 128), f32)
    local[0].wait()
    pl.semaphore_wait(barrier, len(peers))

    def copy(src, dst, send, recv, device):
        made = pltpu.make_async_remote_copy(
            src_ref=src, dst_ref=dst, send_sem=send, recv_sem=recv, device_id=device, device_id_type=MESH
        )
        made.start()
        return made

    def finish(copies):
        for made in copies:
            made.wait_send()
            made.wait_recv()

    ring_right, ring_left, swaps = {}, {}, []

    def ring_step(k):
        spot = blocks.at[block_at(1 - k)]
        ring_right[k] = copy(spot, spot, er_send.at[k], er_recv.at[k], at_z(1))
        if k < 8:
            spot = blocks.at[block_at(k - 1)]
            ring_left[k] = copy(spot, spot, el_send.at[k], el_recv.at[k], at_z(15))

    def swap(d):
        spot = blocks.at[block_at(d)]
        swaps.append(copy(spot, spot, ec_send.at[d % 16], ec_recv.at[d % 16], partner))

    def advance(k):
        ring_right[k].wait_recv()
        if k < 8:
            ring_left[k].wait_recv()
            ring_step(k + 1)
            swap(k)
        swap(-k)

    ring_step(1)
    swap(0)

    for made in local[1:]:
        made.wait()
    fulls = (full_q, full_g, full_d)
    for full, g, e in zip(fulls, (qg, gg, dg), (qe, ge, de)):
        full[...] = g[0].astype(f32) + e[0]
    starts = (0, cols[0], cols[0] + cols[1])
    for m, b in enumerate((qb, gb, db)):
        basis[:, starts[m] : starts[m] + cols[m]] = b[...]
    lands = (land_q, land_g, land_d, land_v)
    for land, w, m in zip(lands, (qw, gw, dw), (qm, gm, dm)):
        land[y] = w[0, 0] - (step_size * momentum_decay) * m[0, 0]
    land_v[y] = vec[...]
    early = []

    def send_early():
        for k, land in enumerate(lands):
            for d in (1, 2, 3):
                early.append(copy(land.at[y], land.at[y], u_send.at[k, d], u_recv.at[k, d], at_y(d)))

    def gather_ids():
        finish(swaps)
        for b in range(32):
            pair = blocks[b, per : per + 16, :].astype(f32)[0:1, :]
            id_rows[b // 4, :, (b % 4) * per : (b % 4 + 1) * per] = pair[:, :per] + 256.0 * pair[:, per:]

    def sum_rows(d, target):
        owner = (y + d) % 4
        spots = lax.broadcasted_iota(jnp.int32, (256, 4 * per), 0) + (s * 4 + owner) * block_rows
        spots = spots.astype(f32)

        def group(g, carry):
            one_hot = jnp.where(spots == id_rows[g], 1.0, 0.0).astype(jnp.bfloat16)
            values = blocks[pl.ds(4 * g, 4), :per, :].reshape(4 * per, 2 * per)
            target[...] += jnp.dot(one_hot, values, preferred_element_type=f32)
            return carry

        target[...] = jnp.zeros(target.shape, f32)
        lax.fori_loop(0, 8, group, 0)

    parts, embs = [], []

    def send_parts():
        for d in (1, 2, 3):
            parts.append(copy(part_send.at[d - 1], part_land.at[d - 1], p_send.at[d], p_recv.at[d], at_y(d)))

    def update_rows():
        finish(parts)
        total = (part_own[...] + part_land[0]) + (part_land[1] + part_land[2])
        moment = momentum_decay * em[...] + total[:block_rows] * 0.25
        emb_moment_out[...] = moment
        emb_land[y, :block_rows] = ew[...] - step_size * moment
        emb_land[y, block_rows:] = jnp.zeros((256 - block_rows, 2 * per), f32)
        for d in (1, 2, 3):
            embs.append(copy(emb_land.at[y], emb_land.at[y], e_send.at[d], e_recv.at[d], at_y(d)))

    def first_ids():
        gather_ids()
        sum_rows(1, part_send.at[0])

    def ring_and_early():
        advance(5)
        send_early()

    beside = {(0, k): (lambda k=k: advance(k + 1)) for k in range(8)}
    beside[0, 4] = ring_and_early
    beside[1, 0] = first_ids
    beside[1, 1] = lambda: sum_rows(2, part_send.at[1])
    beside[1, 2] = lambda: sum_rows(3, part_send.at[2])
    beside[1, 3] = lambda: sum_rows(0, part_own)
    beside[1, 4] = send_parts
    beside[1, 6] = update_rows

    def phase(r, k, copies):
        if (r, k) in beside:
            beside[r, k]()
        finish(copies)

    for r in range(ROUNDS):
        for m in range(3):
            part = dot_nt(basis[:, starts[m] : starts[m] + cols[m]], fulls[m][...])
            xbuf[r, x, m, :, : rows[m]] = part
        phase(r, 0, [copy(xbuf.at[r, x], xbuf.at[r, x], x_send.at[r, d], x_recv.at[r, d], at_x(d)) for d in (1, 2, 3)])
        ybuf[r, y] = (xbuf[r, 0] + xbuf[r, 1]) + (xbuf[r, 2] + xbuf[r, 3])
        phase(r, 1, [copy(ybuf.at[r, y], ybuf.at[r, y], y_send.at[r, d], y_recv.at[r, d], at_y(d)) for d in (1, 2, 3)])
        left = (ybuf[r, 0] + ybuf[r, 1]) + (ybuf[r, 2] + ybuf[r, 3])
        for m in range(3):
            raw = dot_nn(left[m][:, : rows[m]], fulls[m][...])
            for c in range(cols[m] // 128):
                wide[r, :, starts[m] // 128 + c] = raw[:, c * 128 : (c + 1) * 128].reshape(4, 8, 128)
            gram = dot_nt(left[m], left[m]) * 0.25
            wide[r, :, GRAM_CHUNK + m, :, :RANK] = gram.reshape(4, 8, RANK)
        phase(r, 2, [copy(wide.at[r, :, pl.ds(other * 16, 16)], from_core.at[r], c_send.at[r], c_recv.at[r], partner)])
        half[r] = wide[r, :, pl.ds(core * 16, 16)] + from_core[r]
        phase(r, 3, [
            copy(half.at[r, (y + d) % 4], from_y.at[r, d - 1], ry_send.at[r, d], ry_recv.at[r, d], at_y(d))
            for d in (1, 2, 3)
        ])
        mine[r] = (half[r, y] + from_y[r, 0]) + (from_y[r, 1] + from_y[r, 2])
        phase(r, 4, [
            copy(mine.at[r, (z + d) % 16], from_z.at[r, d - 1], rz_send.at[r, d], rz_recv.at[r, d], at_z(d))
            for d in range(1, 16)
        ])
        tiles = [mine[r, z]] + [from_z[r, k] for k in range(15)]
        while len(tiles) > 1:
            tiles = [tiles[k] + tiles[k + 1] for k in range(0, len(tiles), 2)]
        whole[r, core, y, z] = tiles[0]
        spot = whole.at[r, core, y, z]
        phase(r, 5, [copy(spot, spot, gz_send.at[r, d], gz_recv.at[r, d], at_z(d)) for d in range(1, 16)])
        spot_y = whole.at[r, core, y]
        phase(r, 6, [copy(spot_y, spot_y, gy_send.at[r, d], gy_recv.at[r, d], at_y(d)) for d in (1, 2, 3)])
        spot_c = whole.at[r, core]
        phase(r, 7, [copy(spot_c, spot_c, gc_send.at[r], gc_recv.at[r], partner)])
        grams = [whole[r, 1, :, GRAM_CHUNK - 16 + m].reshape(RANK, 128) for m in range(3)]
        inverses = inverse_factors(grams)
        for m in range(3):
            first = starts[m] // 128
            chunks = [
                whole[r, c // 16, :, c % 16].reshape(RANK, 128) for c in range(first, first + cols[m] // 128)
            ]
            basis[:, starts[m] : starts[m] + cols[m]] = dot_nn(inverses[m], jnp.concatenate(chunks, axis=1))
    for m, approx in enumerate((approx_q, approx_g, approx_d)):
        ortho = dot_nn(inverses[m], left[m])
        ortho = ortho.T[: rows[m], :]
        approx[...] = dot_nn(ortho, basis[:, starts[m] : starts[m] + cols[m]]) * 0.25
    finish(early)
    gath_q[...] = land_q[...]
    gath_g[...] = land_g[...]
    gath_d[...] = land_d[...]
    vec_sum[...] = (land_v[0] + land_v[1]) + (land_v[2] + land_v[3])
    for made in list(ring_right.values()) + list(ring_left.values()):
        made.wait_send()
    finish(embs)
    for k in range(4):
        emb_out[k] = emb_land[k, :block_rows]


def power_sgd(matrices, emb_grad, emb_weight, emb_moment, emb_ids, vec_tile):
    rows = tuple(matrix[0].shape[1] for matrix in matrices)
    cols = tuple(matrix[0].shape[2] for matrix in matrices)
    block_rows, width = emb_weight.shape
    per = emb_ids.shape[1]
    far = [operand for matrix in matrices for operand in matrix] + [emb_grad, emb_weight, emb_moment]
    f32 = jnp.float32
    shards = [matrix[3].shape[2:] for matrix in matrices]
    out_shape = [jax.ShapeDtypeStruct((rows[m], cols[m]), f32) for m in range(3)]
    out_shape += [jax.ShapeDtypeStruct((4,) + shape, f32) for shape in shards]
    out_shape += [jax.ShapeDtypeStruct((8, 128), f32)]
    out_shape += [jax.ShapeDtypeStruct((4, block_rows, width), f32), jax.ShapeDtypeStruct((block_rows, width), f32)]
    dma = pltpu.SemaphoreType.DMA
    scratch = [pltpu.VMEM(operand.shape, operand.dtype) for matrix in matrices for operand in matrix]
    scratch += [pltpu.VMEM((block_rows, width), f32)] * 2
    scratch += [pltpu.VMEM((rows[m], cols[m]), f32) for m in range(3)]
    scratch += [pltpu.VMEM((RANK, sum(cols)), f32)]
    scratch += [pltpu.VMEM((4,) + shape, f32) for shape in shards]
    scratch += [
        pltpu.VMEM((4, 8, 128), f32),
        pltpu.VMEM((ROUNDS, 4, 3, RANK, 128), f32),
        pltpu.VMEM((ROUNDS, 4, 3, RANK, 128), f32),
        pltpu.VMEM((ROUNDS, 4, 32, 8, 128), f32),
        pltpu.VMEM((ROUNDS, 4, 16, 8, 128), f32),
        pltpu.VMEM((ROUNDS, 4, 16, 8, 128), f32),
        pltpu.VMEM((ROUNDS, 3, 16, 8, 128), f32),
        pltpu.VMEM((ROUNDS, 16, 8, 128), f32),
        pltpu.VMEM((ROUNDS, 15, 8, 128), f32),
        pltpu.VMEM((ROUNDS, 2, 4, 16, 8, 128), f32),
        pltpu.VMEM((32, per + 16, width), jnp.bfloat16),
        pltpu.VMEM((8, 1, 4 * per), f32),
        pltpu.VMEM((256, width), f32),
        pltpu.VMEM((3, 256, width), f32),
        pltpu.VMEM((3, 256, width), f32),
        pltpu.VMEM((4, 256, width), f32),
        dma((18,)),
    ]
    for shape in (
        (4, 4), (ROUNDS, 4), (ROUNDS, 4), (ROUNDS,), (ROUNDS, 4), (ROUNDS, 16), (ROUNDS, 16), (ROUNDS, 4), (ROUNDS,),
        (9,), (9,), (16,), (4,), (4,),
    ):
        scratch += [dma(shape), dma(shape)]
    vmem = pl.BlockSpec(memory_space=pltpu.VMEM)

    def body(*refs):
        sgd_kernel(rows, cols, block_rows, *refs)

    return pl.pallas_call(
        body,
        out_shape=out_shape,
        in_specs=[pl.BlockSpec(memory_space=pl.ANY)] * len(far) + [vmem] * 2,
        out_specs=[vmem] * len(out_shape),
        scratch_shapes=scratch,
        compiler_params=pltpu.CompilerParams(collective_id=0, has_side_effects=True),
        name="power_sgd",
    )(*far, emb_ids, vec_tile)


def on_device(
    qkv_grad, qkv_error, qkv_basis, qkv_weight, qkv_moment,
    gu_grad, gu_error, gu_basis, gu_weight, gu_moment,
    down_grad, down_error, down_basis, down_weight, down_moment,
    vec_grad, vec_weight, vec_moment,
    emb_ids, emb_grad, emb_weight, emb_moment,
):
    rep_count = lax.axis_size("rep")
    rep_index = lax.axis_index("rep")
    moments = (qkv_moment[0, 0], gu_moment[0, 0], down_moment[0, 0])
    vec_len = vec_weight.shape[0]
    vec_tile = jnp.pad(vec_grad.astype(jnp.float32), ((0, 7), (0, 128 - vec_len)))
    outs = power_sgd(
        (
            (qkv_grad, qkv_error, qkv_basis.T, qkv_weight, qkv_moment),
            (gu_grad, gu_error, gu_basis.T, gu_weight, gu_moment),
            (down_grad, down_error, down_basis.T, down_weight, down_moment),
        ),
        emb_grad, emb_weight[0, 0], emb_moment[0, 0], emb_ids, vec_tile,
    )
    approxes, olds, vec_sum, emb_new, emb_moment_new = outs[:3], outs[3:6], outs[6], outs[7], outs[8]
    results = []
    for index, (grad, error) in enumerate(((qkv_grad, qkv_error), (gu_grad, gu_error), (down_grad, down_error))):
        approx = approxes[index]
        error_new = (grad[0].astype(jnp.float32) + error[0] - approx)[None]
        local_rows = moments[index].shape[0]
        own_rows = lax.dynamic_slice_in_dim(approx, rep_index * local_rows, local_rows, 0)
        moment_new = (momentum_decay * moments[index] + own_rows)[None, None]
        plain = olds[index].reshape(approx.shape) - step_size * approx
        results += [plain, error_new, moment_new]
    vec_mean = vec_sum[0, :vec_len] / rep_count
    vec_moment_new = momentum_decay * vec_moment + vec_mean
    vec_new = vec_weight - step_size * vec_moment_new
    emb_new = emb_new.reshape(-1, emb_new.shape[-1])
    return (*results, vec_new, vec_moment_new, emb_new, emb_moment_new[None, None])


def solution(mesh):
    grouped = P("shard", "rep", None, "tp")
    matrix = P("rep", "shard", "tp")
    per_matrix = (matrix, matrix, P("tp", None), grouped, grouped)
    vector = P(("shard", "tp"))
    return jax.shard_map(
        on_device,
        mesh=mesh,
        in_specs=per_matrix * 3
        + (P("rep", ("shard", "tp")), vector, vector, P("rep", "shard"), matrix, grouped, grouped),
        out_specs=(P("shard", "tp"), matrix, grouped) * 3 + (vector, vector, P("shard", "tp"), grouped),
        check_vma=False,
    )
```

time: 209 us -> 130 us (0.62); the launches traced: 205 us -> 130 us
  waiting for transfers between devices: 29.5 us -> 0 us
  between operations: 14.1 us -> 0.75 us
  blocking collectives: 12.5 us -> 0 us
  Pallas kernels: 123 us -> 115 us
  other arithmetic: 15.9 us -> 8.67 us
  local copies, waits for them, and re-layouts: 10 us -> 5.22 us
    all_gather x1 -> x0, waiting for transfers between devices: 29.5 us -> none  [on_device(): gathered = lax.all_gather(sent, ('rep', 'shard'), axis=0, tiled=True)]
    all_gather x1 -> x0, blocking collectives: 12.5 us -> none  [on_device(): emb_whole = lax.all_gather(emb_flat_new, 'rep', axis=1, tiled=True)]
    pallas_call x2 -> x1, Pallas kernels: 123 us -> 115 us  [power_sgd(): pl.pallas_call(body, out_shape=out_shape, in_specs=[pl.BlockSpec(memory_s...]
    unnamed x25 -> x36, local copies, waits for them, and re-layouts: 9.94 us -> 4.15 us
    sub x4 -> x0, other arithmetic: 3.06 us -> none  [the longest x3 2.42 us: on_device(): w - step_size * momentum_decay * m]
  transfers between devices with their start and end apart: 1 -> 0, of which waited for: 1 -> 0; matrix products, arithmetic and copies ran while one was open for 5% -> 0% of each run, Pallas kernels for 54% -> 0%
where the time goes in v2:
time: 130 us
  Pallas kernels  115 us (88%)
  other arithmetic  8.67 us (7%)
  local copies, waits for them, and re-layouts  5.22 us (4%)
    pallas_call x1, Pallas kernels, power_sgd(): pl.pallas_call(body, out_shape=out_shape, in_specs=[pl.BlockSpec(memory_s...  115 us
    broadcast_in_dim x3, other arithmetic, on_device(): error_new = (grad[0].astype(jnp.float32) + error[0] - approx)[None]  4.23 us
    unnamed x36, local copies, waits for them, and re-layouts  4.15 us
    broadcast_in_dim x3, other arithmetic, on_device(): moment_new = (momentum_decay * moments[index] + own_rows)[None, None]  2.62 us

profile of v2, /device:TPU:1, one launch (start us, length us, event | category | flops | bytes accessed | tf_op | source)
XLA Modules:
  0.0 129.7 jit_solution(4194713141735319160)
XLA Ops:
  0.7 0.0 copy-start.14
  0.7 0.6 copy-done.14
  1.3 0.6 pad_convert_fusion.refs_19_
  1.9 1.9 %copy_bitcast_fusion = (f32[250,256]{1,0:T(8,128)}, f32[250,256]{1,0:T(8,128)}) fusion(f32[1,1,250,256]{3,1,2,0:T(1,128)} %param.43, f32[1,1,250,256]{3,1,2,0:T(1,128)} %param.42), kind=kLoop, calls=%fused_computation | loop fusion | bytes 1024000
  3.8 0.0 copy-start.15
  3.8 0.0 copy-start.16
  3.8 0.0 copy-start.13
  3.8 0.0 copy-start.11
  3.8 0.0 copy-start.12
  3.8 115.1 %power_sgd.1 = (f32[32,768]{1,0:T(8,128)}, f32[32,2048]{1,0:T(8,128)}, f32[128,256]{1,0:T(8,128)}, f32[4,8,768]{2,1,0:T(8,128)}, f32[4,8,2048]{2,1,0:T(8,128)}, ...) custom-call(bf16[1,32,768]{2,1,0:T(8,128)(2,1)} %refs_0_.1, ...), custom_call_target="tpu_custom_call" | custom-call | tf_op jit(solution)/shard_map/power_sgd/pallas_call | solution.py:327
  118.9 0.0 copy-start.5
  118.9 0.0 copy-done.15
  118.9 0.0 copy-done.16
  119.0 1.2 multiply_subtract_fusion
  120.2 0.0 copy-done.13
  120.2 1.3 %fusion.5 = f32[1,1,8,768]{3,2,1,0:T(8,128)} fusion(f32[32,768]{1,0:T(8,128)} %get-tuple-element.23, s32[]{:T(128)S(6)} %select_n.7, f32[1,1,8,768]{3,2,1,0:T(8,128)S(1)} %copy-done.13), kind=kLoop, calls=%fused_computation.16 | loop fusion | flops 12288 | bytes 73732 | tf_op jit(solution)/shard_map/broadcast_in_dim | solution.py:365
  121.5 0.0 copy-done.11
  121.5 0.0 copy-done.5
  121.5 0.0 copy-start.10
  121.5 0.0 copy-start.2
  121.5 0.0 copy-start.8
  121.6 1.7 %fusion.2 = (f32[1,32,768]{2,1,0:T(8,128)}, f32[32,768]{1,0:T(8,128)}) fusion(f32[32,768]{1,0:T(8,128)} %get-tuple-element.23, f32[1,32,768]{2,1,0:T(8,128)S(1)} %copy-done.5, bf16[1,32,768]{2,1,0:T(8,128)(2,1)S(1)} %copy-done.11, f32[4,8,768]{2,1,0:T(8,128)} %get-tuple-element.22), kind=kLoop, calls=%fused_computation.9 | loop fusion | flops 122880 | bytes 540672 | tf_op jit(solution)/shard_map/broadcast_in_dim | solution.py:362
  123.3 0.0 copy-start.9
  123.3 0.0 copy-done.12
  123.3 0.0 copy-done.10
  123.3 0.6 fusion.4
  123.9 0.0 copy-done.2
  123.9 0.2 copy-done.9
  124.1 0.0 copy-start.4
  124.1 0.0 copy-start.6
  124.1 0.0 copy-start.1
  124.1 1.7 %fusion.1 = (f32[1,128,256]{2,1,0:T(8,128)}, f32[128,256]{1,0:T(8,128)}) fusion(f32[128,256]{1,0:T(8,128)S(1)} %copy-done.10, f32[1,128,256]{2,1,0:T(8,128)S(1)} %copy-done.2, bf16[1,128,256]{2,1,0:T(8,128)(2,1)S(1)} %copy-done.9, f32[4,32,256]{2,1,0:T(8,128)} %get-tuple-element.26), kind=kLoop, calls=%fused_computation.6 | loop fusion | flops 163840 | bytes 720896 | tf_op jit(solution)/shard_map/broadcast_in_dim | solution.py:362
  125.8 0.0 copy-start.3
  125.8 0.0 copy-done.4
  125.8 0.0 copy-done.6
  125.8 0.0 copy-start
  125.8 0.6 fusion.3
  126.5 0.0 copy-done.8
  126.5 0.0 copy-done.1
  126.5 0.3 copy-done.3
  126.7 0.0 copy-start.7
  126.7 0.8 fusion
  127.6 0.1 copy-done.7
  127.7 1.0 copy.36
  128.7 0.0 copy-done
  128.7 1.1 reshape.55
Async XLA Ops:
  0.7 0.7 copy-start.14
  3.8 115.1 %copy-start.15 = (f32[88]{0:T(128)S(1)}, f32[88]{0:T(128)}, u32[]{:S(2)}) copy-start(f32[88]{0:T(128)} %param.38) | copy-start | bytes 1060
  3.8 115.2 %copy-start.16 = (f32[88]{0:T(128)S(1)}, f32[88]{0:T(128)}, u32[]{:S(2)}) copy-start(f32[88]{0:T(128)} %param.39) | copy-start | bytes 1060
  3.8 116.4 %copy-start.13 = (f32[1,1,8,768]{3,2,1,0:T(8,128)S(1)}, f32[1,1,8,768]{3,2,1,0:T(8,128)}, u32[]{:S(2)}) copy-start(f32[1,1,8,768]{3,2,1,0:T(8,128)} %refs_4_.1) | copy-start | bytes 73732
  3.8 117.7 %copy-start.11 = (bf16[1,32,768]{2,1,0:T(8,128)(2,1)S(1)}, bf16[1,32,768]{2,1,0:T(8,128)(2,1)}, u32[]{:S(2)}) copy-start(bf16[1,32,768]{2,1,0:T(8,128)(2,1)} %refs_0_.1) | copy-start | bytes 147460
  3.8 119.4 %copy-start.12 = (f32[1,1,32,256]{3,2,1,0:T(8,128)S(1)}, f32[1,1,32,256]{3,2,1,0:T(8,128)}, u32[]{:S(2)}) copy-start(f32[1,1,32,256]{3,2,1,0:T(8,128)} %refs_14_.1) | copy-start | bytes 98308
  118.9 2.6 %copy-start.5 = (f32[1,32,768]{2,1,0:T(8,128)S(1)}, f32[1,32,768]{2,1,0:T(8,128)}, u32[]{:S(2)}) copy-start(f32[1,32,768]{2,1,0:T(8,128)} %refs_1_.1) | copy-start | bytes 294916
  121.5 1.7 %copy-start.10 = (f32[128,256]{1,0:T(8,128)S(1)}, f32[128,256]{1,0:T(8,128)}, u32[]{:S(2)}) copy-start(f32[128,256]{1,0:T(8,128)} %get-tuple-element.27) | copy-start | bytes 393220
  121.5 2.4 %copy-start.2 = (f32[1,128,256]{2,1,0:T(8,128)S(1)}, f32[1,128,256]{2,1,0:T(8,128)}, u32[]{:S(2)}) copy-start(f32[1,128,256]{2,1,0:T(8,128)} %refs_11_.1) | copy-start | bytes 393220
  121.5 4.9 %copy-start.8 = (f32[4,8,2048]{2,1,0:T(8,128)S(1)}, f32[4,8,2048]{2,1,0:T(8,128)}, u32[]{:S(2)}) copy-start(f32[4,8,2048]{2,1,0:T(8,128)} %get-tuple-element.24) | copy-start | bytes 786436
  123.3 0.8 copy-start.9
  124.1 1.7 %copy-start.4 = (f32[32,2048]{1,0:T(8,128)S(1)}, f32[32,2048]{1,0:T(8,128)}, u32[]{:S(2)}) copy-start(f32[32,2048]{1,0:T(8,128)} %get-tuple-element.25) | copy-start | bytes 786436
  124.1 1.7 %copy-start.6 = (f32[1,1,8,2048]{3,2,1,0:T(8,128)S(1)}, f32[1,1,8,2048]{3,2,1,0:T(8,128)}, u32[]{:S(2)}) copy-start(f32[1,1,8,2048]{3,2,1,0:T(8,128)} %refs_9_.1) | copy-start | bytes 196612
  124.1 2.4 %copy-start.1 = (f32[1,32,2048]{2,1,0:T(8,128)S(1)}, f32[1,32,2048]{2,1,0:T(8,128)}, u32[]{:S(2)}) copy-start(f32[1,32,2048]{2,1,0:T(8,128)} %refs_6_.1) | copy-start | bytes 786436
  125.8 0.9 copy-start.3
  125.8 2.9 %copy-start = (f32[4,250,256]{2,1,0:T(8,128)S(1)}, f32[4,250,256]{2,1,0:T(8,128)}, u32[]{:S(2)}) copy-start(f32[4,250,256]{2,1,0:T(8,128)} %get-tuple-element.29) | copy-start | bytes 3072004
  126.7 1.0 copy-start.7

commit v3 on v2

--- a/solution.py
+++ b/solution.py
@@ -47,15 +47,15 @@
     (
         qg_hbm, qe_hbm, qb_hbm, qw_hbm, qm_hbm, gg_hbm, ge_hbm, gb_hbm, gw_hbm, gm_hbm,
         dg_hbm, de_hbm, db_hbm, dw_hbm, dm_hbm, rows_hbm, ew_hbm, em_hbm, ids, vec,
-        approx_q, approx_g, approx_d, gath_q, gath_g, gath_d, vec_sum, emb_out, emb_moment_out,
+        new_q, new_g, new_d, err_q, err_g, err_d, mom_q, mom_g, mom_d, vec_sum, emb_out, emb_moment_out,
         qg, qe, qb, qw, qm, gg, ge, gb, gw, gm, dg, de, db, dw, dm, ew, em,
         full_q, full_g, full_d, basis, land_q, land_g, land_d, land_v,
         xbuf, ybuf, wide, half, from_core, from_y, mine, from_z, whole,
-        blocks, id_rows, part_own, part_send, part_land, emb_land,
+        blocks, id_rows, part_own, part_send, part_mid, part_land, emb_land,
         l_sem,
         u_send, u_recv, x_send, x_recv, y_send, y_recv, c_send, c_recv,
         ry_send, ry_recv, rz_send, rz_recv, gz_send, gz_recv, gy_send, gy_recv, gc_send, gc_recv,
-        er_send, er_recv, el_send, el_recv, ec_send, ec_recv, p_send, p_recv, e_send, e_recv,
+        er_send, er_recv, el_send, el_recv, ec_send, ec_recv, h_send, h_recv, p_send, p_recv, e_send, e_recv, f_send, f_recv,
     ) = refs
     f32 = jnp.float32
     y = lax.axis_index("rep")
@@ -102,9 +102,6 @@
         xbuf[r, x] = jnp.zeros(xbuf.shape[2:], f32)
         for c in range(GRAM_CHUNK, 32):
             wide[r, :, c] = jnp.zeros((4, 8, 128), f32)
-    local[0].wait()
-    pl.semaphore_wait(barrier, len(peers))
-
     def copy(src, dst, send, recv, device):
         made = pltpu.make_async_remote_copy(
             src_ref=src, dst_ref=dst, send_sem=send, recv_sem=recv, device_id=device, device_id_type=MESH
@@ -138,21 +135,20 @@
             swap(k)
         swap(-k)
 
-    ring_step(1)
-    swap(0)
-
-    for made in local[1:]:
+    for made in local:
         made.wait()
     fulls = (full_q, full_g, full_d)
     for full, g, e in zip(fulls, (qg, gg, dg), (qe, ge, de)):
         full[...] = g[0].astype(f32) + e[0]
     starts = (0, cols[0], cols[0] + cols[1])
+    spans = ((0, rows[0]), (rows[0], rows[0] + rows[1]), (0, rows[2]))
     for m, b in enumerate((qb, gb, db)):
         basis[:, starts[m] : starts[m] + cols[m]] = b[...]
     lands = (land_q, land_g, land_d, land_v)
     for land, w, m in zip(lands, (qw, gw, dw), (qm, gm, dm)):
         land[y] = w[0, 0] - (step_size * momentum_decay) * m[0, 0]
-    land_v[y] = vec[...]
+    land_v[y] = jnp.zeros((8, 128), f32)
+    land_v[y, 0:1, : vec.shape[1]] = vec[...].astype(f32)
     early = []
 
     def send_early():
@@ -180,38 +176,57 @@
         target[...] = jnp.zeros(target.shape, f32)
         lax.fori_loop(0, 8, group, 0)
 
-    parts, embs = [], []
+    halves, parts, embs, tails = [], [], [], []
+
+    def send_halves():
+        halves.append(copy(part_send.at[1, pl.ds(0, 128)], part_mid.at[0], h_send.at[0], h_recv.at[0], at_y(1)))
+        halves.append(copy(part_send.at[1, pl.ds(128, 128)], part_mid.at[1], h_send.at[1], h_recv.at[1], at_y(3)))
 
     def send_parts():
-        for d in (1, 2, 3):
-            parts.append(copy(part_send.at[d - 1], part_land.at[d - 1], p_send.at[d], p_recv.at[d], at_y(d)))
+        finish(halves)
+        part_send[0, :128] += part_mid[0]
+        part_send[2, 128:] += part_mid[1]
+        parts.append(copy(part_send.at[0], part_land.at[0], p_send.at[0], p_recv.at[0], at_y(1)))
+        parts.append(copy(part_send.at[2], part_land.at[1], p_send.at[1], p_recv.at[1], at_y(3)))
 
     def update_rows():
         finish(parts)
-        total = (part_own[...] + part_land[0]) + (part_land[1] + part_land[2])
-        moment = momentum_decay * em[...] + total[:block_rows] * 0.25
+        total = part_own[...] + (part_land[0] + part_land[1])
+        moment = momentum_decay * em[...].reshape(block_rows, 2 * per) + total[:block_rows] * 0.25
         emb_moment_out[...] = moment
-        emb_land[y, :block_rows] = ew[...] - step_size * moment
+        emb_land[y, :block_rows] = ew[...].reshape(block_rows, 2 * per) - step_size * moment
         emb_land[y, block_rows:] = jnp.zeros((256 - block_rows, 2 * per), f32)
-        for d in (1, 2, 3):
-            embs.append(copy(emb_land.at[y], emb_land.at[y], e_send.at[d], e_recv.at[d], at_y(d)))
+        embs.append(copy(emb_land.at[y], emb_land.at[y], e_send.at[0], e_recv.at[0], at_y(1)))
+        embs.append(copy(emb_land.at[y], emb_land.at[y], e_send.at[1], e_recv.at[1], at_y(3)))
+
+    def forward_rows():
+        finish(embs)
+        spot = emb_land.at[(y + 3) % 4, pl.ds(0, 128)]
+        tails.append(copy(spot, spot, f_send.at[0], f_recv.at[0], at_y(1)))
+        spot = emb_land.at[(y + 1) % 4, pl.ds(128, 128)]
+        tails.append(copy(spot, spot, f_send.at[1], f_recv.at[1], at_y(3)))
 
     def first_ids():
         gather_ids()
-        sum_rows(1, part_send.at[0])
+        sum_rows(2, part_send.at[1])
 
     def ring_and_early():
         advance(5)
         send_early()
 
+    def third_rows():
+        send_halves()
+        sum_rows(3, part_send.at[2])
+
     beside = {(0, k): (lambda k=k: advance(k + 1)) for k in range(8)}
     beside[0, 4] = ring_and_early
     beside[1, 0] = first_ids
-    beside[1, 1] = lambda: sum_rows(2, part_send.at[1])
-    beside[1, 2] = lambda: sum_rows(3, part_send.at[2])
+    beside[1, 1] = lambda: sum_rows(1, part_send.at[0])
+    beside[1, 2] = third_rows
     beside[1, 3] = lambda: sum_rows(0, part_own)
     beside[1, 4] = send_parts
-    beside[1, 6] = update_rows
+    beside[1, 5] = update_rows
+    beside[1, 6] = forward_rows
 
     def phase(r, k, copies):
         if (r, k) in beside:
@@ -221,13 +236,18 @@
     for r in range(ROUNDS):
         for m in range(3):
             part = dot_nt(basis[:, starts[m] : starts[m] + cols[m]], fulls[m][...])
-            xbuf[r, x, m, :, : rows[m]] = part
+            xbuf[r, x, m // 2, :, spans[m][0] : spans[m][1]] = part
+        if r == 0:
+            pl.semaphore_wait(barrier, len(peers))
+            ring_step(1)
+            swap(0)
         phase(r, 0, [copy(xbuf.at[r, x], xbuf.at[r, x], x_send.at[r, d], x_recv.at[r, d], at_x(d)) for d in (1, 2, 3)])
         ybuf[r, y] = (xbuf[r, 0] + xbuf[r, 1]) + (xbuf[r, 2] + xbuf[r, 3])
         phase(r, 1, [copy(ybuf.at[r, y], ybuf.at[r, y], y_send.at[r, d], y_recv.at[r, d], at_y(d)) for d in (1, 2, 3)])
-        left = (ybuf[r, 0] + ybuf[r, 1]) + (ybuf[r, 2] + ybuf[r, 3])
+        both = (ybuf[r, 0] + ybuf[r, 1]) + (ybuf[r, 2] + ybuf[r, 3])
+        left = [both[m // 2][:, spans[m][0] : spans[m][1]] for m in range(3)]
         for m in range(3):
-            raw = dot_nn(left[m][:, : rows[m]], fulls[m][...])
+            raw = dot_nn(left[m], fulls[m][...])
             for c in range(cols[m] // 128):
                 wide[r, :, starts[m] // 128 + c] = raw[:, c * 128 : (c + 1) * 128].reshape(4, 8, 128)
             gram = dot_nt(left[m], left[m]) * 0.25
@@ -261,44 +281,47 @@
                 whole[r, c // 16, :, c % 16].reshape(RANK, 128) for c in range(first, first + cols[m] // 128)
             ]
             basis[:, starts[m] : starts[m] + cols[m]] = dot_nn(inverses[m], jnp.concatenate(chunks, axis=1))
-    for m, approx in enumerate((approx_q, approx_g, approx_d)):
-        ortho = dot_nn(inverses[m], left[m])
-        ortho = ortho.T[: rows[m], :]
-        approx[...] = dot_nn(ortho, basis[:, starts[m] : starts[m] + cols[m]]) * 0.25
     finish(early)
-    gath_q[...] = land_q[...]
-    gath_g[...] = land_g[...]
-    gath_d[...] = land_d[...]
+    outs = ((new_q, err_q, mom_q, qm), (new_g, err_g, mom_g, gm), (new_d, err_d, mom_d, dm))
+    for m, (new, err, mom, old) in enumerate(outs):
+        ortho = dot_nn(inverses[m], left[m]).T
+        approx = dot_nn(ortho, basis[:, starts[m] : starts[m] + cols[m]]) * 0.25
+        err[0] = fulls[m][...] - approx
+        new[...] = approx
+        own = old.shape[2]
+        mom[0, 0] = momentum_decay * old[0, 0] + new[pl.ds(pl.multiple_of(y * own, own), own), :]
+        new[...] = lands[m][...].reshape(rows[m], cols[m]) - step_size * approx
     vec_sum[...] = (land_v[0] + land_v[1]) + (land_v[2] + land_v[3])
     for made in list(ring_right.values()) + list(ring_left.values()):
         made.wait_send()
-    finish(embs)
+    finish(tails)
     for k in range(4):
-        emb_out[k] = emb_land[k, :block_rows]
+        emb_out[k * block_rows : (k + 1) * block_rows, :] = emb_land[k, :block_rows]
 
 
 def power_sgd(matrices, emb_grad, emb_weight, emb_moment, emb_ids, vec_tile):
     rows = tuple(matrix[0].shape[1] for matrix in matrices)
     cols = tuple(matrix[0].shape[2] for matrix in matrices)
-    block_rows, width = emb_weight.shape
+    block_rows, _, width = emb_weight.shape
     per = emb_ids.shape[1]
     far = [operand for matrix in matrices for operand in matrix] + [emb_grad, emb_weight, emb_moment]
     f32 = jnp.float32
     shards = [matrix[3].shape[2:] for matrix in matrices]
     out_shape = [jax.ShapeDtypeStruct((rows[m], cols[m]), f32) for m in range(3)]
-    out_shape += [jax.ShapeDtypeStruct((4,) + shape, f32) for shape in shards]
+    out_shape += [jax.ShapeDtypeStruct((1, rows[m], cols[m]), f32) for m in range(3)]
+    out_shape += [jax.ShapeDtypeStruct((1, 1) + shape, f32) for shape in shards]
     out_shape += [jax.ShapeDtypeStruct((8, 128), f32)]
-    out_shape += [jax.ShapeDtypeStruct((4, block_rows, width), f32), jax.ShapeDtypeStruct((block_rows, width), f32)]
+    out_shape += [jax.ShapeDtypeStruct((4 * block_rows, width), f32), jax.ShapeDtypeStruct((block_rows, width), f32)]
     dma = pltpu.SemaphoreType.DMA
     scratch = [pltpu.VMEM(operand.shape, operand.dtype) for matrix in matrices for operand in matrix]
-    scratch += [pltpu.VMEM((block_rows, width), f32)] * 2
+    scratch += [pltpu.VMEM((block_rows, 1, width), f32)] * 2
     scratch += [pltpu.VMEM((rows[m], cols[m]), f32) for m in range(3)]
     scratch += [pltpu.VMEM((RANK, sum(cols)), f32)]
     scratch += [pltpu.VMEM((4,) + shape, f32) for shape in shards]
     scratch += [
         pltpu.VMEM((4, 8, 128), f32),
-        pltpu.VMEM((ROUNDS, 4, 3, RANK, 128), f32),
-        pltpu.VMEM((ROUNDS, 4, 3, RANK, 128), f32),
+        pltpu.VMEM((ROUNDS, 4, 2, RANK, 128), f32),
+        pltpu.VMEM((ROUNDS, 4, 2, RANK, 128), f32),
         pltpu.VMEM((ROUNDS, 4, 32, 8, 128), f32),
         pltpu.VMEM((ROUNDS, 4, 16, 8, 128), f32),
         pltpu.VMEM((ROUNDS, 4, 16, 8, 128), f32),
@@ -310,13 +333,14 @@
         pltpu.VMEM((8, 1, 4 * per), f32),
         pltpu.VMEM((256, width), f32),
         pltpu.VMEM((3, 256, width), f32),
-        pltpu.VMEM((3, 256, width), f32),
+        pltpu.VMEM((2, 128, width), f32),
+        pltpu.VMEM((2, 256, width), f32),
         pltpu.VMEM((4, 256, width), f32),
         dma((18,)),
     ]
     for shape in (
         (4, 4), (ROUNDS, 4), (ROUNDS, 4), (ROUNDS,), (ROUNDS, 4), (ROUNDS, 16), (ROUNDS, 16), (ROUNDS, 4), (ROUNDS,),
-        (9,), (9,), (16,), (4,), (4,),
+        (9,), (9,), (16,), (2,), (2,), (2,), (2,),
     ):
         scratch += [dma(shape), dma(shape)]
     vmem = pl.BlockSpec(memory_space=pltpu.VMEM)
@@ -335,6 +359,33 @@
     )(*far, emb_ids, vec_tile)
 
 
+def place(arrays):
+    count = len(arrays)
+
+    def body(*refs):
+        sources, targets = refs[:count], refs[count : 2 * count]
+        held, load, store = refs[2 * count : 3 * count], refs[3 * count], refs[3 * count + 1]
+        loads = [pltpu.make_async_copy(sources[k], held[k], load.at[k]) for k in range(count)]
+        stores = [pltpu.make_async_copy(held[k], targets[k], store.at[k]) for k in range(count)]
+        for made in loads:
+            made.start()
+        for k in range(count):
+            loads[k].wait()
+            stores[k].start()
+        for made in stores:
+            made.wait()
+
+    far = pl.BlockSpec(memory_space=pl.ANY)
+    return pl.pallas_call(
+        body,
+        out_shape=[jax.ShapeDtypeStruct(a.shape, a.dtype) for a in arrays],
+        in_specs=[far] * count,
+        out_specs=[far] * count,
+        scratch_shapes=[pltpu.VMEM(a.shape, a.dtype) for a in arrays] + [pltpu.SemaphoreType.DMA((count,))] * 2,
+        name="place",
+    )(*arrays)
+
+
 def on_device(
     qkv_grad, qkv_error, qkv_basis, qkv_weight, qkv_moment,
     gu_grad, gu_error, gu_basis, gu_weight, gu_moment,
@@ -343,33 +394,25 @@
     emb_ids, emb_grad, emb_weight, emb_moment,
 ):
     rep_count = lax.axis_size("rep")
-    rep_index = lax.axis_index("rep")
-    moments = (qkv_moment[0, 0], gu_moment[0, 0], down_moment[0, 0])
     vec_len = vec_weight.shape[0]
-    vec_tile = jnp.pad(vec_grad.astype(jnp.float32), ((0, 7), (0, 128 - vec_len)))
+    block_rows, width = emb_weight.shape[2:]
     outs = power_sgd(
         (
             (qkv_grad, qkv_error, qkv_basis.T, qkv_weight, qkv_moment),
             (gu_grad, gu_error, gu_basis.T, gu_weight, gu_moment),
             (down_grad, down_error, down_basis.T, down_weight, down_moment),
         ),
-        emb_grad, emb_weight[0, 0], emb_moment[0, 0], emb_ids, vec_tile,
+        emb_grad, emb_weight.reshape(block_rows, 1, width), emb_moment.reshape(block_rows, 1, width), emb_ids, vec_grad,
     )
-    approxes, olds, vec_sum, emb_new, emb_moment_new = outs[:3], outs[3:6], outs[6], outs[7], outs[8]
-    results = []
-    for index, (grad, error) in enumerate(((qkv_grad, qkv_error), (gu_grad, gu_error), (down_grad, down_error))):
-        approx = approxes[index]
-        error_new = (grad[0].astype(jnp.float32) + error[0] - approx)[None]
-        local_rows = moments[index].shape[0]
-        own_rows = lax.dynamic_slice_in_dim(approx, rep_index * local_rows, local_rows, 0)
-        moment_new = (momentum_decay * moments[index] + own_rows)[None, None]
-        plain = olds[index].reshape(approx.shape) - step_size * approx
-        results += [plain, error_new, moment_new]
+    vec_sum, emb_moment_new = outs[9], outs[11]
+    new_q, new_g, new_d, err_q, err_g, err_d, mom_q, mom_g, mom_d, emb_new = place(list(outs[:9]) + [outs[10]])
     vec_mean = vec_sum[0, :vec_len] / rep_count
     vec_moment_new = momentum_decay * vec_moment + vec_mean
     vec_new = vec_weight - step_size * vec_moment_new
-    emb_new = emb_new.reshape(-1, emb_new.shape[-1])
-    return (*results, vec_new, vec_moment_new, emb_new, emb_moment_new[None, None])
+    return (
+        new_q, err_q, mom_q, new_g, err_g, mom_g, new_d, err_d, mom_d,
+        vec_new, vec_moment_new, emb_new, emb_moment_new[None, None],
+    )
 
 
 def solution(mesh):

time: 130 us -> 120 us (0.923)
  other arithmetic: 8.67 us -> 1.2 us
  local copies, waits for them, and re-layouts: 5.22 us -> 1.62 us
    broadcast_in_dim x6 -> x0, other arithmetic: 6.85 us -> none  [the longest x3 4.23 us: on_device(): error_new = (grad[0].astype(jnp.float32) + error[0] - approx)[None]]
    pallas_call x0 -> x1, Pallas kernels: none -> 2.81 us  [place(): pl.pallas_call(body, out_shape=[jax.ShapeDtypeStruct(a.shape, a.dtype) fo...]
    unnamed x36 -> x7, local copies, waits for them, and re-layouts: 4.15 us -> 1.62 us
    pallas_call x1, Pallas kernels: 115 us -> 114 us  [power_sgd(): pl.pallas_call(body, out_shape=out_shape, in_specs=[pl.BlockSpec(memory_s...]
where the time goes in v3:
time: 120 us
  Pallas kernels  116 us (97%)
  local copies, waits for them, and re-layouts  1.62 us (1%)
  other arithmetic  1.2 us (1%)
    pallas_call x1, Pallas kernels, power_sgd(): pl.pallas_call(body, out_shape=out_shape, in_specs=[pl.BlockSpec(memory_s...  114 us
    pallas_call x1, Pallas kernels, place(): pl.pallas_call(body, out_shape=[jax.ShapeDtypeStruct(a.shape, a.dtype) fo...  2.81 us

profile of v3, /device:TPU:1, one launch (start us, length us, event | category | flops | bytes accessed | tf_op | source)
XLA Modules:
  0.0 119.9 jit_solution(3512346014959438429)
XLA Ops:
  0.7 113.6 %power_sgd.1 = (f32[32,768]{1,0:T(8,128)}, f32[32,2048]{1,0:T(8,128)}, f32[128,256]{1,0:T(8,128)}, f32[1,32,768]{2,1,0:T(8,128)}, f32[1,32,2048]{2,1,0:T(8,128)}...) custom-call(bf16[1,32,768]{2,1,0:T(8,128)(2,1)} %refs_0_.1, ...), custom_call_target="tpu_custom_call" | custom-call | tf_op jit(solution)/shard_map/power_sgd/pallas_call | solution.py:351
  114.2 0.0 copy-start
  114.3 2.8 %place.1 = (f32[32,768]{1,0:T(8,128)}, f32[32,2048]{1,0:T(8,128)}, f32[128,256]{1,0:T(8,128)}, f32[1,32,768]{2,1,0:T(8,128)}, f32[1,32,2048]{2,1,0:T(8,128)}, /*...) custom-call(f32[32,768]{1,0:T(8,128)} %get-tuple-element.35.refs_0_,, ...), custom_call_target="tpu_custom_call" | custom-call | tf_op jit(solution)/shard_map/place/pallas_call | solution.py:379
  117.1 0.0 copy-start.1
  117.1 0.0 copy-start.2
  117.1 0.6 copy-done.1
  117.7 0.0 copy-done.2
  117.7 1.2 multiply_subtract_fusion
  118.9 0.0 copy-done
  118.9 1.0 copy.35
Async XLA Ops:
  114.2 4.7 %copy-start = (f32[250,256]{1,0:T(8,128)S(1)}, f32[250,256]{1,0:T(8,128)}, u32[]{:S(2)}) copy-start(f32[250,256]{1,0:T(8,128)} %get-tuple-element.56) | copy-start | bytes 768004
  117.1 0.7 copy-start.1
  117.1 0.7 copy-start.2

commit v4 on v3

--- a/solution.py
+++ b/solution.py
@@ -7,7 +7,8 @@
 
 ROUNDS = 2
 RANK = 32
-GRAM_CHUNK = 24
+HALF = 12
+USED = 15
 
 momentum_decay = 0.9
 step_size = 0.05
@@ -100,8 +101,10 @@
     blocks[core * 16 + z, per : per + 16, :] = digits
     for r in range(ROUNDS):
         xbuf[r, x] = jnp.zeros(xbuf.shape[2:], f32)
-        for c in range(GRAM_CHUNK, 32):
+        mine[r, USED] = jnp.zeros((8, 128), f32)
+        for c in range(HALF, USED):
             wide[r, :, c] = jnp.zeros((4, 8, 128), f32)
+            wide[r, :, 16 + c] = jnp.zeros((4, 8, 128), f32)
     def copy(src, dst, send, recv, device):
         made = pltpu.make_async_remote_copy(
             src_ref=src, dst_ref=dst, send_sem=send, recv_sem=recv, device_id=device, device_id_type=MESH
@@ -214,17 +217,17 @@
         advance(5)
         send_early()
 
-    def third_rows():
-        send_halves()
-        sum_rows(3, part_send.at[2])
+    def parts_and_own():
+        send_parts()
+        sum_rows(0, part_own)
 
     beside = {(0, k): (lambda k=k: advance(k + 1)) for k in range(8)}
     beside[0, 4] = ring_and_early
     beside[1, 0] = first_ids
     beside[1, 1] = lambda: sum_rows(1, part_send.at[0])
-    beside[1, 2] = third_rows
-    beside[1, 3] = lambda: sum_rows(0, part_own)
-    beside[1, 4] = send_parts
+    beside[1, 2] = send_halves
+    beside[1, 3] = lambda: sum_rows(3, part_send.at[2])
+    beside[1, 4] = parts_and_own
     beside[1, 5] = update_rows
     beside[1, 6] = forward_rows
 
@@ -249,16 +252,20 @@
         for m in range(3):
             raw = dot_nn(left[m], fulls[m][...])
             for c in range(cols[m] // 128):
-                wide[r, :, starts[m] // 128 + c] = raw[:, c * 128 : (c + 1) * 128].reshape(4, 8, 128)
+                chunk = starts[m] // 128 + c
+                wide[r, :, chunk // HALF * 16 + chunk % HALF] = raw[:, c * 128 : (c + 1) * 128].reshape(4, 8, 128)
             gram = dot_nt(left[m], left[m]) * 0.25
-            wide[r, :, GRAM_CHUNK + m, :, :RANK] = gram.reshape(4, 8, RANK)
-        phase(r, 2, [copy(wide.at[r, :, pl.ds(other * 16, 16)], from_core.at[r], c_send.at[r], c_recv.at[r], partner)])
-        half[r] = wide[r, :, pl.ds(core * 16, 16)] + from_core[r]
+            wide[r, :, HALF + m, :, :RANK] = gram.reshape(4, 8, RANK)
+            wide[r, :, 16 + HALF + m, :, :RANK] = gram.reshape(4, 8, RANK)
+        phase(r, 2, [
+            copy(wide.at[r, :, pl.ds(other * 16, USED)], from_core.at[r], c_send.at[r], c_recv.at[r], partner)
+        ])
+        half[r] = wide[r, :, pl.ds(core * 16, USED)] + from_core[r]
         phase(r, 3, [
             copy(half.at[r, (y + d) % 4], from_y.at[r, d - 1], ry_send.at[r, d], ry_recv.at[r, d], at_y(d))
             for d in (1, 2, 3)
         ])
-        mine[r] = (half[r, y] + from_y[r, 0]) + (from_y[r, 1] + from_y[r, 2])
+        mine[r, :USED] = (half[r, y] + from_y[r, 0]) + (from_y[r, 1] + from_y[r, 2])
         phase(r, 4, [
             copy(mine.at[r, (z + d) % 16], from_z.at[r, d - 1], rz_send.at[r, d], rz_recv.at[r, d], at_z(d))
             for d in range(1, 16)
@@ -269,23 +276,26 @@
         whole[r, core, y, z] = tiles[0]
         spot = whole.at[r, core, y, z]
         phase(r, 5, [copy(spot, spot, gz_send.at[r, d], gz_recv.at[r, d], at_z(d)) for d in range(1, 16)])
-        spot_y = whole.at[r, core, y]
+        spot_y = whole.at[r, core, y, pl.ds(0, USED)]
         phase(r, 6, [copy(spot_y, spot_y, gy_send.at[r, d], gy_recv.at[r, d], at_y(d)) for d in (1, 2, 3)])
-        spot_c = whole.at[r, core]
-        phase(r, 7, [copy(spot_c, spot_c, gc_send.at[r], gc_recv.at[r], partner)])
-        grams = [whole[r, 1, :, GRAM_CHUNK - 16 + m].reshape(RANK, 128) for m in range(3)]
-        inverses = inverse_factors(grams)
+        spot_c = whole.at[r, core, :, pl.ds(0, USED)]
+        last = copy(spot_c, spot_c, gc_send.at[r], gc_recv.at[r], partner)
+        if (r, 7) in beside:
+            beside[r, 7]()
+        inverses = inverse_factors([whole[r, core, :, HALF + m].reshape(RANK, 128) for m in range(3)])
+        if r == ROUNDS - 1:
+            orthos = [dot_nn(inverses[m], left[m]).T for m in range(3)]
+        finish([last])
         for m in range(3):
             first = starts[m] // 128
             chunks = [
-                whole[r, c // 16, :, c % 16].reshape(RANK, 128) for c in range(first, first + cols[m] // 128)
+                whole[r, c // HALF, :, c % HALF].reshape(RANK, 128) for c in range(first, first + cols[m] // 128)
             ]
             basis[:, starts[m] : starts[m] + cols[m]] = dot_nn(inverses[m], jnp.concatenate(chunks, axis=1))
     finish(early)
     outs = ((new_q, err_q, mom_q, qm), (new_g, err_g, mom_g, gm), (new_d, err_d, mom_d, dm))
     for m, (new, err, mom, old) in enumerate(outs):
-        ortho = dot_nn(inverses[m], left[m]).T
-        approx = dot_nn(ortho, basis[:, starts[m] : starts[m] + cols[m]]) * 0.25
+        approx = dot_nn(orthos[m], basis[:, starts[m] : starts[m] + cols[m]]) * 0.25
         err[0] = fulls[m][...] - approx
         new[...] = approx
         own = old.shape[2]
@@ -323,9 +333,9 @@
         pltpu.VMEM((ROUNDS, 4, 2, RANK, 128), f32),
         pltpu.VMEM((ROUNDS, 4, 2, RANK, 128), f32),
         pltpu.VMEM((ROUNDS, 4, 32, 8, 128), f32),
-        pltpu.VMEM((ROUNDS, 4, 16, 8, 128), f32),
-        pltpu.VMEM((ROUNDS, 4, 16, 8, 128), f32),
-        pltpu.VMEM((ROUNDS, 3, 16, 8, 128), f32),
+        pltpu.VMEM((ROUNDS, 4, USED, 8, 128), f32),
+        pltpu.VMEM((ROUNDS, 4, USED, 8, 128), f32),
+        pltpu.VMEM((ROUNDS, 3, USED, 8, 128), f32),
         pltpu.VMEM((ROUNDS, 16, 8, 128), f32),
         pltpu.VMEM((ROUNDS, 15, 8, 128), f32),
         pltpu.VMEM((ROUNDS, 2, 4, 16, 8, 128), f32),

time: 120 us -> 115 us (0.958)
  Pallas kernels: 116 us -> 111 us
    pallas_call x1, Pallas kernels: 114 us -> 108 us  [power_sgd(): pl.pallas_call(body, out_shape=out_shape, in_specs=[pl.BlockSpec(memory_s...]
where the time goes in v4:
time: 115 us
  Pallas kernels  111 us (97%)
  local copies, waits for them, and re-layouts  1.62 us (1%)
  other arithmetic  1.2 us (1%)
    pallas_call x1, Pallas kernels, power_sgd(): pl.pallas_call(body, out_shape=out_shape, in_specs=[pl.BlockSpec(memory_s...  108 us
    pallas_call x1, Pallas kernels, place(): pl.pallas_call(body, out_shape=[jax.ShapeDtypeStruct(a.shape, a.dtype) fo...  2.81 us

profile of v4, /device:TPU:1, one launch (start us, length us, event | category | flops | bytes accessed | tf_op | source)
XLA Modules:
  0.0 114.5 jit_solution(18263957924024201898)
XLA Ops:
  0.7 108.2 %power_sgd.1 = (f32[32,768]{1,0:T(8,128)}, f32[32,2048]{1,0:T(8,128)}, f32[128,256]{1,0:T(8,128)}, f32[1,32,768]{2,1,0:T(8,128)}, f32[1,32,2048]{2,1,0:T(8,128)}...) custom-call(bf16[1,32,768]{2,1,0:T(8,128)(2,1)} %refs_0_.1, ...), custom_call_target="tpu_custom_call" | custom-call | tf_op jit(solution)/shard_map/power_sgd/pallas_call | solution.py:361
  108.9 0.0 copy-start
  108.9 2.8 %place.1 = (f32[32,768]{1,0:T(8,128)}, f32[32,2048]{1,0:T(8,128)}, f32[128,256]{1,0:T(8,128)}, f32[1,32,768]{2,1,0:T(8,128)}, f32[1,32,2048]{2,1,0:T(8,128)}, /*...) custom-call(f32[32,768]{1,0:T(8,128)} %get-tuple-element.35.refs_0_,, ...), custom_call_target="tpu_custom_call" | custom-call | tf_op jit(solution)/shard_map/place/pallas_call | solution.py:389
  111.7 0.0 copy-start.1
  111.7 0.0 copy-start.2
  111.7 0.6 copy-done.1
  112.4 0.0 copy-done.2
  112.4 1.2 %multiply_subtract_fusion = (f32[88]{0:T(128)}, f32[88]{0:T(128)}) fusion(f32[88]{0:T(128)S(1)} %copy-done.1, f32[8,128]{1,0:T(8,128)} %get-tuple-element.54, f32[88]{0:T(128)S(1)} %copy-done.2), kind=kLoop, calls=%fused_computation.1 | loop fusion | flops 440 | bytes 1760 | tf_op jit(solution)/shard_map/sub | solution.py:421
  113.6 0.0 copy-done
  113.6 1.0 copy.35
Async XLA Ops:
  108.9 4.7 %copy-start = (f32[250,256]{1,0:T(8,128)S(1)}, f32[250,256]{1,0:T(8,128)}, u32[]{:S(2)}) copy-start(f32[250,256]{1,0:T(8,128)} %get-tuple-element.56) | copy-start | bytes 768004
  111.7 0.7 copy-start.1
  111.7 0.7 copy-start.2
